TPU v7x, 256 devices: a whole 4x4x8 slice. The times are simulated.
256 devices in a mesh: row: 8 (over z), col: 16 (over y, x), pan: 2 (over core).
Axes of the slice: x: 4, y: 4, z: 8, core: 2. Of those that a mesh axis runs over, the one named last changes fastest.
Arguments:
- plan_values: bfloat16 [8192, 128, 256], P('row', 'col', 'pan'), may hold values from 0.099609375 to 1
- plan_blocks: int32 [8, 128], P('row', 'col'), may hold values from 0 to 127, as said below
- first_values: bfloat16 [32, 3, 256, 256], P('row'), may hold values from -0.21875 to 0.21875
- first_blocks: int32 [32, 3], P('row'), may hold values from 0 to 3, as said below
- second_values: bfloat16 [128, 6, 256, 256], P('col', None, None, 'pan'), may hold values from -0.15625 to 0.15625
- second_blocks: int32 [128, 6], P('col'), may hold values from 0 to 7, as said below
- weight_first: float32 [8192], P('row'), may hold values from 0.5 to 2
- weight_second: float32 [128, 256], P('col', 'pan'), may hold values from 0.5 to 2
- offset_first: float32 [8192], P('row'), may hold values from -3 to 3
- offset_second: float32 [128, 256], P('col', 'pan'), may hold values from -3 to 3
Outputs:
- new_plan: bfloat16 [8192, 128, 256], P('row', 'col', 'pan')
- scale_first: float32 [8192], P('row')
- scale_second: float32 [128, 256], P('col', 'pan')
Inputs may be any that keep to these rules, and one draw needn't show every extreme that they name: `plan_blocks`: each entry is a slice-B block number; its column panel is the entry // 8. Within the 8 slots of one index of col (aligned groups of the second dimension) no column panel is named more than 2 times, and in every row panel one column panel is named exactly 2 times by every such group. `first_blocks`: block numbers within the row panel of the slice-A block; the 3 entries of a row are distinct. `second_blocks`: block numbers within the column panel of the slice-B block; the 6 entries of a row are distinct.
All inputs are finite; a program needn't handle non-finite values.
Results may differ from a plain program's by a relative error of at most 0.0087.
Values may be sent and summed in bfloat16 or wider, within the bound.
No kernel may reach another device: no remote copies, remote signals or barrier semaphores. Data moves between devices by JAX's collectives and lax.ppermute only.
A program may use at most 128 MiB of HBM per device.

v0:
```python
import jax
import jax.numpy as jnp
from jax import lax
from jax.sharding import PartitionSpec as P

CAP = 2


def first_product(plan_values, first_values, first_blocks):
    tile_count = first_blocks.shape[0]
    block_size = first_values.shape[2]
    slot_count = plan_values.shape[1]
    half_width = plan_values.shape[2]
    row_tiles = plan_values.reshape(tile_count, block_size, slot_count * half_width)
    running = jnp.zeros(row_tiles.shape, jnp.float32)
    for neighbor in range(first_blocks.shape[1]):
        picked = jnp.take(row_tiles, first_blocks[:, neighbor], axis=0)
        running = running + jnp.einsum(
            "iab,ibn->ian", first_values[:, neighbor], picked, preferred_element_type=jnp.float32
        )
    return running.astype(jnp.bfloat16).reshape(tile_count * block_size, slot_count, half_width)


def dispatch(chooser, within_panel, product):
    outgoing = jnp.einsum(
        "dcs,rsh->dcrh", chooser.astype(jnp.bfloat16), product, preferred_element_type=jnp.float32
    ).astype(jnp.bfloat16)
    labels = jnp.sum(chooser.astype(jnp.int32) * (within_panel + 1)[None, None, :], axis=2) - 1
    return (outgoing, labels)


def second_product(dense_plan, second_values, second_blocks):
    blocks_here = second_blocks.shape[0]
    columns = jnp.arange(blocks_here)
    placer = (second_blocks[:, :, None] == columns[None, None, :]).astype(jnp.bfloat16)
    panel_matrix = jnp.einsum(
        "kqbh,kql->kblh", second_values, placer, preferred_element_type=jnp.float32
    ).astype(jnp.bfloat16)
    return jnp.einsum("rkb,kblh->rlh", dense_plan, panel_matrix, preferred_element_type=jnp.float32)


def local(
    plan_values,
    plan_blocks,
    first_values,
    first_blocks,
    second_values,
    second_blocks,
    weight_first,
    weight_second,
    offset_first,
    offset_second,
):
    col_count = lax.axis_size("col")
    blocks_here = second_blocks.shape[0]
    slot_count = plan_values.shape[1]
    block_size = first_values.shape[2]
    panel_rows = plan_values.shape[0]
    plan_width = float(slot_count * col_count * block_size)
    named_blocks = plan_blocks[0]
    target_panel = named_blocks // blocks_here
    within_panel = named_blocks % blocks_here
    same_panel = target_panel[:, None] == target_panel[None, :]
    earlier = jnp.arange(slot_count)[:, None] > jnp.arange(slot_count)[None, :]
    position = jnp.sum((same_panel & earlier).astype(jnp.int32), axis=1)
    chooser = (target_panel[None, None, :] == jnp.arange(col_count)[:, None, None]) & (
        position[None, None, :] == jnp.arange(CAP)[None, :, None]
    )
    product = first_product(plan_values, first_values, first_blocks)
    outgoing, labels = dispatch(chooser, within_panel, product)
    incoming, arrival_ids = (
        lax.all_to_all(outgoing, "col", split_axis=0, concat_axis=0, tiled=True),
        lax.all_to_all(labels, "col", split_axis=0, concat_axis=0, tiled=True),
    )
    item_rows = incoming.shape[2]
    arrivals = incoming.reshape(col_count * CAP, item_rows, incoming.shape[3])
    matcher = (arrival_ids.reshape(-1)[:, None] == jnp.arange(blocks_here)[None, :]).astype(
        jnp.bfloat16
    )
    dense_plan = jnp.einsum(
        "ik,irh->rkh", matcher, arrivals, preferred_element_type=jnp.float32
    ).astype(jnp.bfloat16)
    present = jnp.minimum(jnp.sum(matcher.astype(jnp.float32), axis=0), 1.0)
    gathered = lax.all_gather(dense_plan, "pan", axis=2, tiled=True)
    crossed = second_product(gathered, second_values, second_blocks)
    kernel_values = present[None, :, None] * jnp.exp(
        crossed - offset_first[:, None, None] - offset_second[None]
    )
    row_totals = lax.psum(jnp.sum(kernel_values, axis=(1, 2)), ("col", "pan"))
    scale_first = weight_first * plan_width / row_totals
    weighted = kernel_values * scale_first[:, None, None]
    colsum, counts = lax.psum((jnp.sum(weighted, axis=0), present * float(panel_rows)), "row")
    scale_second = weight_second * counts[:, None] / jnp.where(counts[:, None] > 0, colsum, 1.0)
    new_values = (weighted * scale_second[None]).astype(jnp.bfloat16)
    returned = jnp.einsum(
        "ik,rkh->irh", matcher, new_values, preferred_element_type=jnp.float32
    ).astype(jnp.bfloat16)
    returned = returned.reshape(col_count, CAP, item_rows, returned.shape[2])
    homeward = lax.all_to_all(returned, "col", split_axis=0, concat_axis=0, tiled=True)
    new_plan = jnp.einsum(
        "dcs,dcrh->rsh", chooser.astype(jnp.bfloat16), homeward, preferred_element_type=jnp.float32
    ).astype(jnp.bfloat16)
    return (new_plan, scale_first, scale_second)


def solution(mesh):
    return jax.shard_map(
        local,
        mesh=mesh,
        in_specs=(
            P("row", "col", "pan"),
            P("row", "col"),
            P("row", None, None, None),
            P("row", None),
            P("col", None, None, "pan"),
            P("col", None),
            P("row"),
            P("col", "pan"),
            P("row"),
            P("col", "pan"),
        ),
        out_specs=(P("row", "col", "pan"), P("row"), P("col", "pan")),
        check_vma=False,
    )
```

profile of v0, /device:TPU:32, one launch (start us, length us, event | category | flops | bytes accessed | tf_op | source)
XLA Modules:
  0.0 441.3 jit_solution(4532502949180978923)
XLA Ops:
  7.2 0.0 copy-start
  7.2 0.8 fusion.59
  8.0 0.8 fusion.60
  8.8 0.1 iota_compare_fusion.3
  8.9 0.2 convert_reduce_fusion.1
  9.1 0.1 fusion.47
  9.2 0.7 copy.46
  9.8 7.0 %all-to-all-start = ((s32[16,1,2]{2,1,0:T(1,128)}), s32[16,1,2]{2,1,0:T(1,128)S(1)}, u32[]{:S(2)}, u32[]{:S(2)}) async-start(s32[16,1,2]{2,1,0:T(1,128)} %copy.46), calls=%async_computation | async-start | bytes 16384 | tf_op jit(solution)/shard_map/all_to_all | solution.py:73
  16.9 1.0 slice_reduce_fusion.1
  18.0 4.2 reshape.172
  22.1 3.6 gather_fusion.1
  25.7 3.6 gather_fusion.2
  29.3 3.6 gather_fusion
  32.9 2.8 fusion.20
  35.7 0.0 copy-done.3
  35.8 1.0 fusion.22
  36.8 0.5 copy-done.2
  37.4 2.7 fusion.29
  40.0 4.0 copy.53
  44.0 2.2 copy.72
  46.3 5.2 %convolution_convert_fusion.1 = bf16[16,2,1024,128]{3,0,2,1:T(8,128)(2,1)} fusion(bf16[1024,8,128,1]{2,1,0,3:T(8,128)(2,1)S(1)} %bitcast.93, pred[2,8]{1,0:T(4,128)(4,1)S(1)} %iota_compare_fusion.4, pred[16,8]{0,1:T(8,128)(4,1)S(1)} %iota_compare_fusion.3), kind=kOutput, calls=%fused_computation.8 | convolution fusion | flops 71303424 | bytes 10485904 | tf_op jit(solution)/shard_map/dcs,rsh->dcrh/dot_general | solution.py:25
  51.4 8.8 %copy.54 = bf16[16,2,1024,128]{3,2,1,0:T(8,128)(2,1)} copy(bf16[16,2,1024,128]{3,0,2,1:T(8,128)(2,1)} %convolution_convert_fusion.1) | data formatting | bytes 16777216 | tf_op jit(solution)/shard_map/convert_element_type | solution.py:27
  60.2 0.0 all-to-all-done
  60.2 7.3 %all-to-all-start.1 = ((bf16[16,2,1024,128]{3,2,1,0:T(8,128)(2,1)}), bf16[16,2,1024,128]{3,2,1,0:T(8,128)(2,1)}, u32[]{:S(2)}, u32[]{:S(2)}) async-start(bf16[16,2,1024,128]{3,2,1,0:T(8,128)(2,1)} %copy.54), calls=%async_computation.1 | async-start | bytes 16777216 | tf_op jit(solution)/shard_map/all_to_all | solution.py:72
  67.5 0.2 all-gather.2.cloned.1.call-start
  67.7 0.5 broadcast.270
  68.2 0.7 reduce.9
  68.9 0.1 eq.91
  69.0 121.1 %all-to-all-done.1 = bf16[16,2,1024,128]{3,2,1,0:T(8,128)(2,1)} async-done(((bf16[16,2,1024,128]{3,2,1,0:T(8,128)(2,1)}), bf16[16,2,1024,128]{3,2,1,0:T(8,128)(2,1)}, u32[]{:S(2)}, u32[]{:S(2)}) %all-to-all-start.1) | async-done | bytes 8388640 | tf_op jit(solution)/shard_map/all_to_all | solution.py:72
  190.0 9.3 %convert_bitcast_fusion.1 = bf16[1024,8,128]{2,1,0:T(8,128)(2,1)} fusion(bf16[32,1024,128]{2,1,0:T(8,128)(2,1)} %bitcast.10, s32[32]{0:T(128)S(1)} %eq.91), kind=kOutput, calls=%fused_computation.31 | convolution fusion | flops 68157696 | bytes 10485888 | tf_op jit(solution)/shard_map/ik,irh->rkh/dot_general | solution.py:80
  199.3 0.0 all-gather.2.cloned.1.call-update
  199.4 0.0 copy-start.7
  199.4 0.0 copy-start.8
  199.4 4.0 convert_bitcast_fusion
  203.4 0.1 convert_reduce_fusion
  203.5 15.7 %all-gather.2.cloned.1.call-done = bf16[1024,8,256]{2,1,0:T(8,128)(2,1)} async-done(((bf16[1024,8,128]{2,1,0:T(8,128)(2,1)}), bf16[1024,8,256]{2,1,0:T(8,128)(2,1)}) %all-gather.2.cloned.1.call-update) | async-done | bytes 4194320 | tf_op jit(solution)/shard_map/all_gather | solution.py:84
  219.2 10.1 %fusion.15 = (f32[1024]{0:T(1024)S(1)}, f32[1024,8,128,1]{2,0,3,1:T(8,128)}) fusion(f32[8,128]{1,0:T(8,128)S(1)} %copy-done.7, f32[1024]{0:T(1024)S(1)} %copy-done.8, f32[8]{0:T(128)S(1)} %get-tuple-element.10, bf16[8,256,8,128]{3,2,1,0:T(8,128)(2,1)} %convert_bitcast_fusion, bf16[1024,8,256]{2,1,0:T(8,128)(2,1)} %all-gather.2.cloned.1.call-done), kind=kOutput, calls=%fused_computation.24 | convolution fusion | flops 4299160576 | bytes 12595232 | tf_op jit(solution)/shard_map/rkb,kblh->rlh/dot_general | solution.py:39
  229.3 67.6 %psum.21 = f32[1024]{0:T(1024)S(1)} all-reduce(f32[1024]{0:T(1024)S(1)} %get-tuple-element.13), channel_id=1, replica_groups=mesh['row'=8,'col'=16,'pan'=2] {'col','pan'}, use_global_device_ids=true, to_apply=%region_4.6 | all-reduce | flops 1024 | bytes 8192 | tf_op jit(solution)/shard_map/psum | solution.py:89
  296.9 0.0 copy-start.5
  296.9 3.3 multiply_reduce_fusion
  300.2 16.3 %all-reduce = (f32[8,128]{1,0:T(8,128)S(1)}, f32[8]{0:T(128)S(1)}) all-reduce(f32[8,128]{1,0:T(8,128)S(1)} %multiply_reduce_fusion, f32[8]{0:T(128)S(1)} %get-tuple-element.9), channel_id=1, replica_groups=mesh['row'=8,'col'=16,'pan'=2] {'row'}, use_global_device_ids=true, to_apply=%region_7.9 | all-reduce | flops 1032 | bytes 8256 | tf_op jit(solution)/shard_map/psum | solution.py:92
  316.5 0.1 select_divide_fusion
  316.6 3.8 multiply_convert_fusion
  320.5 6.3 %convolution_convert_fusion = bf16[32,1024,128]{2,0,1:T(8,128)(2,1)S(1)} fusion(bf16[1024,8,128]{2,0,1:T(8,128)(2,1)S(1)} %multiply_convert_fusion, s32[32]{0:T(128)S(1)} %eq.91), kind=kOutput, calls=%fused_computation.7 | convolution fusion | flops 71303424 | bytes 10485888 | tf_op jit(solution)/shard_map/ik,rkh->irh/dot_general | solution.py:95
  326.8 8.0 %copy.60 = bf16[16,2,1024,128]{3,1,2,0:T(2,128)(2,1)S(1)} copy(bf16[16,2,1024,128]{3,1,0,2:T(2,128)(2,1)S(1)} %bitcast.91) | data formatting | bytes 16777216 | tf_op jit(solution)/shard_map/reshape | solution.py:98
  334.8 0.0 copy-start.1
  334.8 93.6 %all_to_all.16 = bf16[16,2,1024,128]{3,1,2,0:T(2,128)(2,1)S(1)} all-to-all(bf16[16,2,1024,128]{3,1,2,0:T(2,128)(2,1)S(1)} %copy.60), channel_id=1, replica_groups=mesh['row'=8,'col'=16,'pan'=2] {'col'}, dimensions={0} | all-to-all | bytes 16777216 | tf_op jit(solution)/shard_map/all_to_all | solution.py:99
  428.5 6.0 %fusion.32 = bf16[1024,8,128]{2,1,0:T(8,128)(2,1)} fusion(bf16[16,2,1024,128]{3,1,2,0:T(2,128)(2,1)S(1)} %all_to_all.16, pred[2,8]{1,0:T(4,128)(4,1)S(1)} %iota_compare_fusion.4, pred[16,8]{0,1:T(8,128)(4,1)S(1)} %iota_compare_fusion.3), kind=kOutput, calls=%fused_computation.36 | convolution fusion | flops 68157696 | bytes 10485904 | tf_op jit(solution)/shard_map/dcs,dcrh->rsh/dot_general | solution.py:100
  (29 shorter events, 0.1 us)
Async XLA Ops:
  7.2 192.2 %copy-start = (bf16[8,6,256,128]{3,2,1,0:T(8,128)(2,1)S(1)}, bf16[8,6,256,128]{3,2,1,0:T(8,128)(2,1)}, u32[]{:S(2)}) copy-start(bf16[8,6,256,128]{3,2,1,0:T(8,128)(2,1)} %param.16) | copy-start | bytes 9437188
  9.8 50.3 %all-to-all-start = ((s32[16,1,2]{2,1,0:T(1,128)}), s32[16,1,2]{2,1,0:T(1,128)S(1)}, u32[]{:S(2)}, u32[]{:S(2)}) async-start(s32[16,1,2]{2,1,0:T(1,128)} %copy.46), calls=%async_computation | async-start | bytes 16384 | tf_op jit(solution)/shard_map/all_to_all | solution.py:73
  32.9 2.8 copy-start.3
  32.9 2.8 copy-start.4
  35.8 1.6 copy-start.2
  60.2 129.8 %all-to-all-start.1 = ((bf16[16,2,1024,128]{3,2,1,0:T(8,128)(2,1)}), bf16[16,2,1024,128]{3,2,1,0:T(8,128)(2,1)}, u32[]{:S(2)}, u32[]{:S(2)}) async-start(bf16[16,2,1024,128]{3,2,1,0:T(8,128)(2,1)} %copy.54), calls=%async_computation.1 | async-start | bytes 16777216 | tf_op jit(solution)/shard_map/all_to_all | solution.py:72
  67.5 151.7 %all-gather.2.cloned.1.call-start = ((), (), s32[]{:S(2)}) async-start(), calls=%async_computation.3 | async-start | bytes 6291456 | tf_op jit(solution)/shard_map/all_gather | solution.py:84
  190.0 9.4 %copy-start.9 = (s32[8,6]{1,0:T(8,128)S(1)}, s32[8,6]{1,0:T(8,128)}, u32[]{:S(2)}) copy-start(s32[8,6]{1,0:T(8,128)} %param.17) | copy-start | bytes 580
  199.4 19.8 %copy-start.7 = (f32[8,128]{1,0:T(8,128)S(1)}, f32[8,128]{1,0:T(8,128)}, u32[]{:S(2)}) copy-start(f32[8,128]{1,0:T(8,128)} %param.21) | copy-start | bytes 12292
  199.4 19.8 %copy-start.8 = (f32[1024]{0:T(1024)S(1)}, f32[1024]{0:T(1024)}, u32[]{:S(2)}) copy-start(f32[1024]{0:T(1024)} %param.20) | copy-start | bytes 12292
  219.2 77.7 %copy-start.10 = (f32[1024]{0:T(1024)S(1)}, f32[1024]{0:T(1024)}, u32[]{:S(2)}) copy-start(f32[1024]{0:T(1024)} %param.18) | copy-start | bytes 12292
  229.3 87.2 %copy-start.11 = (f32[8,128]{1,0:T(8,128)S(1)}, f32[8,128]{1,0:T(8,128)}, u32[]{:S(2)}) copy-start(f32[8,128]{1,0:T(8,128)} %param.19) | copy-start | bytes 12292
  296.9 23.6 %copy-start.5 = (f32[1024]{0:T(1024)}, f32[1024]{0:T(1024)S(1)}, u32[]{:S(2)}) copy-start(f32[1024]{0:T(1024)S(1)} %multiply_divide_fusion) | copy-start | bytes 12292
  316.6 10.2 %copy-start.6 = (f32[8,128]{1,0:T(8,128)}, f32[8,128]{1,0:T(8,128)S(1)}, u32[]{:S(2)}) copy-start(f32[8,128]{1,0:T(8,128)S(1)} %select_divide_fusion) | copy-start | bytes 12292
  334.8 99.6 %copy-start.1 = (bf16[8,6,256,128]{3,2,1,0:T(8,128)(2,1)S(1)}, bf16[8,6,256,128]{3,2,1,0:T(8,128)(2,1)}, u32[]{:S(2)}) copy-start(bf16[8,6,256,128]{3,2,1,0:T(8,128)(2,1)} %param.16) | copy-start | bytes 9437188
Sparse Core Ops, SparseCore 0:
  199.5 19.6 all-gather.1
where the time goes:
time: 443 us; the launch traced here: 441 us
  blocking collectives  178 us (40%)
  waiting for transfers between devices  137 us (31%)
  matrix products  47.4 us (11%)
  local copies, waits for them, and re-layouts  40.8 us (9%)
  starting transfers between devices  14.5 us (3%)
  between operations  14.3 us (3%)
  other arithmetic  10 us (2%)
    all_to_all x1, waiting for transfers between devices, local(): lax.all_to_all(outgoing, 'col', split_axis=0, concat_axis=0, tiled=True)  121 us
    all_to_all x1, blocking collectives, local(): lax.all_to_all(returned, 'col', split_axis=0, concat_axis=0, tiled=True)  93.6 us
    psum x1, blocking collectives, local(): row_totals = lax.psum(jnp.sum(kernel_values, axis=(1, 2)), ('col', 'pan'))  67.6 us
    psum x1, blocking collectives, local(): lax.psum((jnp.sum(weighted, axis=0), present * float(panel_rows)), 'row')  16.3 us
    all_gather x1, waiting for transfers between devices, local(): gathered = lax.all_gather(dense_plan, 'pan', axis=2, tiled=True)  15.7 us
    gather x3, local copies, waits for them, and re-layouts, first_product(): picked = jnp.take(row_tiles, first_blocks[:, neighbor], axis=0)  10.8 us
    dot_general x1, matrix products, second_product(): jnp.einsum('rkb,kblh->rlh', dense_plan, panel_matrix, preferred_element_t...  10.1 us
    dot_general x1, matrix products, local(): jnp.einsum('ik,irh->rkh', matcher, arrivals, preferred_element_type=jnp.f...  9.33 us
  transfers between devices with their start and end apart: 3, of which 2 were waited for; matrix products, arithmetic and copies ran while one was open for 11% of the time, Pallas kernels for 0%

commit v1 on v0

v1 whole, which is shorter than its diff:
```python
import functools
import jax
import jax.numpy as jnp
from jax import lax
from jax.experimental import pallas as pl
from jax.experimental.pallas import tpu as pltpu
from jax.sharding import PartitionSpec as P

LARGEST = float(jnp.finfo(jnp.bfloat16).max)


def params(mebibytes=40):
    return pltpu.CompilerParams(
        dimension_semantics=("arbitrary",), vmem_limit_bytes=mebibytes << 20
    )


def cost(flops, moved):
    return pl.CostEstimate(flops=flops, bytes_accessed=moved, transcendentals=0)


def first_kernel(near, x_ref, c_ref, o_ref, flat):
    step = pl.program_id(0)
    tiles, rows, width = flat.shape
    slots, half = x_ref.shape[1], x_ref.shape[2]
    chunk = o_ref.shape[2]

    @pl.when(step < tiles)
    def _():
        flat[step] = x_ref[...].reshape(rows, width)

    @pl.when(step >= tiles)
    def _():
        total = None
        for q in range(c_ref.shape[1]):
            term = jnp.dot(
                c_ref[0, q], flat[near[step - tiles, q]], preferred_element_type=jnp.float32
            )
            total = term if total is None else total + term
        total = total.astype(jnp.bfloat16)
        for part in range(o_ref.shape[0]):
            for slot in range(slots):
                o_ref[part, slot] = total[
                    part * chunk : (part + 1) * chunk, slot * half : (slot + 1) * half
                ]


def first_product(x, values, near, col_count):
    panel_rows, slots, half = x.shape
    tiles, count, rows, _ = values.shape
    chunk = panel_rows // col_count
    parts = rows // chunk

    def late(i, n):
        return (jnp.maximum(i - tiles, 0), 0, 0, 0)

    return pl.pallas_call(
        first_kernel,
        grid_spec=pltpu.PrefetchScalarGridSpec(
            num_scalar_prefetch=1,
            grid=(2 * tiles,),
            in_specs=[
                pl.BlockSpec((rows, slots, half), lambda i, n: (jnp.minimum(i, tiles - 1), 0, 0)),
                pl.BlockSpec((1, count, rows, rows), late),
            ],
            out_specs=pl.BlockSpec((parts, slots, chunk, half), late),
            scratch_shapes=[pltpu.VMEM((tiles, rows, slots * half), jnp.bfloat16)],
        ),
        out_shape=jax.ShapeDtypeStruct((col_count, slots, chunk, half), jnp.bfloat16),
        compiler_params=params(60),
        cost_estimate=cost(2 * panel_rows * count * rows * slots * half, 6 << 20),
        name="first_product",
    )(near, x, values)


def panel_kernel(near, place, v_ref, mine_ref, other_ref):
    block = pl.program_id(0)
    half = v_ref.shape[3]
    mine_ref[...] = jnp.zeros_like(mine_ref)
    other_ref[...] = jnp.zeros_like(other_ref)
    mine = pl.multiple_of(place[0] * half, half)
    other = pl.multiple_of((1 - place[0]) * half, half)
    for q in range(v_ref.shape[1]):
        target = pl.ds(pl.multiple_of(near[block, q] * half, half), half)
        mine_ref[:, target] = v_ref[0, q, pl.ds(mine, half), :]
        other_ref[:, target] = v_ref[0, q, pl.ds(other, half), :]


def panel_matrix(values, near, place):
    blocks, count, rows, half = values.shape
    out = pl.BlockSpec((half, blocks * half), lambda i, n, h: (i, 0))
    return pl.pallas_call(
        panel_kernel,
        grid_spec=pltpu.PrefetchScalarGridSpec(
            num_scalar_prefetch=2,
            grid=(blocks,),
            in_specs=[pl.BlockSpec((1, count, rows, half), lambda i, n, h: (i, 0, 0, 0))],
            out_specs=[out, out],
        ),
        out_shape=[jax.ShapeDtypeStruct((blocks * half, blocks * half), jnp.bfloat16)] * 2,
        compiler_params=params(),
        cost_estimate=cost(0, 8 << 20),
        name="panel_matrix",
    )(near, place, values)


def merge_kernel(ids, place, x_ref, o_ref, total):
    total[...] = jnp.zeros_like(total)
    slots = x_ref.shape[1]
    for step in range(x_ref.shape[0]):
        source = step ^ place[0]
        for slot in range(slots):
            total[ids[step * slots + slot]] += x_ref[source, slot].astype(jnp.float32)
    o_ref[...] = total[...].astype(jnp.bfloat16)


def merge(ids, place, x, block_count):
    sources, slots, rows, half = x.shape
    out = (block_count, rows, half)
    return pl.pallas_call(
        merge_kernel,
        grid_spec=pltpu.PrefetchScalarGridSpec(
            num_scalar_prefetch=2,
            grid=(1,),
            in_specs=[pl.BlockSpec(x.shape, lambda i, n, h: (0, 0, 0, 0))],
            out_specs=pl.BlockSpec(out, lambda i, n, h: (0, 0, 0)),
            scratch_shapes=[pltpu.VMEM(out, jnp.float32)],
        ),
        out_shape=jax.ShapeDtypeStruct(out, jnp.bfloat16),
        compiler_params=params(),
        cost_estimate=cost(0, 8 << 20),
        name="merge",
    )(ids, place, x)


def select_kernel(ids, place, x_ref, o_ref):
    slots = o_ref.shape[1]
    for step in range(o_ref.shape[0]):
        source = step ^ place[0]
        for slot in range(slots):
            o_ref[source, slot] = x_ref[ids[step * slots + slot]]


def select(ids, place, x, shape):
    return pl.pallas_call(
        select_kernel,
        grid_spec=pltpu.PrefetchScalarGridSpec(
            num_scalar_prefetch=2,
            grid=(1,),
            in_specs=[pl.BlockSpec(x.shape, lambda i, n, h: (0, 0, 0))],
            out_specs=pl.BlockSpec(shape, lambda i, n, h: (0, 0, 0, 0)),
        ),
        out_shape=pltpu.HBM(shape, jnp.bfloat16),
        compiler_params=params(),
        cost_estimate=cost(0, 4 << 20),
        name="select",
    )(ids, place, x)


def lay(x_ref, left):
    parts, blocks, chunk, half = x_ref.shape
    for part in range(parts):
        for block in range(blocks):
            left[part * chunk : (part + 1) * chunk, block * half : (block + 1) * half] = x_ref[
                part, block
            ]


def near_kernel(x_ref, m_ref, o_ref, left):
    lay(x_ref, left)
    o_ref[...] = jnp.dot(left[...], m_ref[...], preferred_element_type=jnp.float32)


def second_near(x, matrix, parts):
    col_count, blocks, chunk, half = x.shape
    depth, width = matrix.shape
    return pl.pallas_call(
        near_kernel,
        grid=(col_count // parts,),
        in_specs=[
            pl.BlockSpec((parts, blocks, chunk, half), lambda i: (i, 0, 0, 0)),
            pl.BlockSpec((depth, width), lambda i: (0, 0)),
        ],
        out_specs=pl.BlockSpec((parts * chunk, width), lambda i: (i, 0)),
        out_shape=jax.ShapeDtypeStruct((col_count * chunk, width), jnp.float32),
        scratch_shapes=[pltpu.VMEM((parts * chunk, depth), jnp.bfloat16)],
        compiler_params=params(),
        cost_estimate=cost(2 * col_count * chunk * depth * width, 8 << 20),
        name="second_near",
    )(x, matrix)


def far_kernel(x_ref, m_ref, near_ref, first_ref, second_ref, o_ref, sum_ref, left):
    parts, blocks, chunk, half = x_ref.shape
    lay(x_ref, left)
    first = jnp.broadcast_to(first_ref[...], (parts * chunk, half))
    partial = None
    for block in range(0, blocks, 2):
        columns = slice(block * half, (block + 2) * half)
        far = jnp.dot(left[...], m_ref[:, columns], preferred_element_type=jnp.float32)
        for side in range(2):
            own = slice((block + side) * half, (block + side + 1) * half)
            crossed = far[:, side * half : (side + 1) * half] + near_ref[:, own]
            value = jnp.exp(crossed - first - second_ref[:, own])
            partial = value if partial is None else partial + value
            rounded = jnp.minimum(value, LARGEST).astype(jnp.bfloat16)
            for part in range(parts):
                o_ref[part, block + side] = rounded[part * chunk : (part + 1) * chunk]
    sum_ref[0] = jnp.sum(partial.T, axis=0, keepdims=True)


def second_far(x, matrix, near, first, second, parts):
    col_count, blocks, chunk, half = x.shape
    steps = col_count // parts
    depth, width = matrix.shape
    data = pl.BlockSpec((parts, blocks, chunk, half), lambda i: (i, 0, 0, 0))
    return pl.pallas_call(
        far_kernel,
        grid=(steps,),
        in_specs=[
            data,
            pl.BlockSpec((depth, width), lambda i: (0, 0)),
            pl.BlockSpec((parts * chunk, width), lambda i: (i, 0)),
            pl.BlockSpec((parts * chunk, 1), lambda i: (i, 0)),
            pl.BlockSpec((1, width), lambda i: (0, 0)),
        ],
        out_specs=[data, pl.BlockSpec((1, 1, parts * chunk), lambda i: (i, 0, 0))],
        out_shape=[
            pltpu.HBM((col_count, blocks, chunk, half), jnp.bfloat16),
            jax.ShapeDtypeStruct((steps, 1, parts * chunk), jnp.float32),
        ],
        scratch_shapes=[pltpu.VMEM((parts * chunk, depth), jnp.bfloat16)],
        compiler_params=params(),
        cost_estimate=cost(2 * col_count * chunk * depth * width, 10 << 20),
        name="second_far",
    )(x, matrix, near, first, second)


def colsum_kernel(s_ref, x_ref, o_ref):
    parts, blocks, chunk, half = x_ref.shape
    for block in range(blocks):
        total = jnp.dot(
            s_ref[...],
            x_ref[:, block].reshape(parts * chunk, half),
            preferred_element_type=jnp.float32,
        )
        o_ref[block : block + 1] = total[0:1] + total[1:2] + total[2:3]


def weighted_colsum(scale, x):
    col_count, blocks, chunk, half = x.shape
    high = scale.astype(jnp.bfloat16)
    rest = scale - high.astype(jnp.float32)
    middle = rest.astype(jnp.bfloat16)
    low = (rest - middle.astype(jnp.float32)).astype(jnp.bfloat16)
    thirds = jnp.concatenate(
        [high[None], middle[None], low[None], jnp.zeros((13, scale.shape[0]), jnp.bfloat16)]
    )
    return pl.pallas_call(
        colsum_kernel,
        out_shape=jax.ShapeDtypeStruct((blocks, half), jnp.float32),
        compiler_params=pltpu.CompilerParams(vmem_limit_bytes=48 * 1024 * 1024),
        cost_estimate=cost(2 * 16 * col_count * blocks * chunk * half, 4 << 20),
        name="weighted_colsum",
    )(thirds, x)


def final_kernel(lines, x_ref, first_ref, second_ref, o_ref):
    parts, slots, chunk, half = x_ref.shape
    for part in range(parts):
        rows = slice(part * chunk, (part + 1) * chunk)
        first = jnp.broadcast_to(first_ref[rows, :], (chunk, half))
        values = [
            x_ref[part, slot].astype(jnp.float32) * first * second_ref[pl.ds(lines[slot], 1), :]
            for slot in range(slots)
        ]
        o_ref[rows] = jnp.swapaxes(jnp.stack(values), 0, 1).astype(jnp.bfloat16)


def final_scale(named, x, first, second, parts):
    col_count, slots, chunk, half = x.shape
    steps = col_count // parts
    return pl.pallas_call(
        final_kernel,
        grid_spec=pltpu.PrefetchScalarGridSpec(
            num_scalar_prefetch=1,
            grid=(steps,),
            in_specs=[
                pl.BlockSpec((parts, slots, chunk, half), lambda i, n: (i, 0, 0, 0)),
                pl.BlockSpec((parts * chunk, 1), lambda i, n: (i, 0)),
                pl.BlockSpec(second.shape, lambda i, n: (0, 0)),
            ],
            out_specs=pl.BlockSpec((parts * chunk, slots, half), lambda i, n: (i, 0, 0)),
        ),
        out_shape=jax.ShapeDtypeStruct((col_count * chunk, slots, half), jnp.bfloat16),
        compiler_params=params(),
        cost_estimate=cost(0, 5 << 20),
        name="final_scale",
    )(named, x, first, second)


def swap(value, axis, bit):
    size = lax.axis_size(axis)
    return lax.ppermute(value, axis, [(i, i ^ bit) for i in range(size)])


def step_row(value, by, bits):
    rows, cols = lax.axis_size("row"), lax.axis_size("col")
    pairs = [
        (r * cols + c, (r + by) % rows * cols + (c ^ bits))
        for r in range(rows)
        for c in range(cols)
    ]
    return lax.ppermute(value, ("row", "col"), pairs)


def four(value, low, by, same):
    own = value if same else step_row(value, by, 0)
    return [own] + [step_row(value, by, k * low) for k in (1, 2, 3)]


def local(
    plan_values,
    plan_blocks,
    first_values,
    first_blocks,
    second_values,
    second_blocks,
    weight_first,
    weight_second,
    offset_first,
    offset_second,
):
    col_count = lax.axis_size("col")
    column = lax.axis_index("col")
    side = lax.axis_index("pan")
    blocks_here = second_blocks.shape[0]
    panel_rows, slots, half = plan_values.shape
    block_size = first_values.shape[2]
    chunk = panel_rows // col_count
    plan_width = float(slots * col_count * block_size)
    block_count = blocks_here * col_count

    named = plan_blocks[0]
    place = column.reshape(1)
    product = first_product(plan_values, first_values, first_blocks, col_count)
    arrived = lax.all_to_all(product, "col", split_axis=0, concat_axis=0, tiled=True)
    ids = jnp.concatenate(four(named, 1, 1, False))
    ids = jnp.concatenate(four(ids, 4, -1, False))
    matrix_mine, matrix_other = panel_matrix(second_values, second_blocks, side.reshape(1))
    own_blocks = column * blocks_here + jnp.arange(blocks_here)
    present = jnp.any(ids[:, None] == own_blocks[None, :], axis=0)
    ids, matrix_mine, matrix_other = lax.optimization_barrier((ids, matrix_mine, matrix_other))
    merged = merge(ids, place, arrived, block_count)
    merged = merged.reshape(col_count, blocks_here, chunk, half)
    mine = lax.all_to_all(merged, "col", split_axis=0, concat_axis=0, tiled=True)
    other = swap(mine, "pan", 1)
    near = second_near(mine, matrix_mine, 8)
    offsets = jnp.where(present[:, None], offset_second, jnp.inf).reshape(1, -1)
    kernel, totals = second_far(other, matrix_other, near, offset_first[:, None], offsets, 8)
    back = lax.all_to_all(kernel, "col", split_axis=0, concat_axis=0, tiled=True)

    totals = totals.reshape(blocks_here, -1)
    totals = totals + swap(totals, "pan", 1)
    for low, by in ((1, 1), (4, -1)):
        own, one, two, three = four(totals, low, by, False)
        totals = (own + one) + (two + three)
    scale_first = weight_first * plan_width / totals.reshape(-1)
    colsum = weighted_colsum(scale_first, kernel)
    sums = jnp.concatenate(
        [colsum, jnp.broadcast_to(present.astype(jnp.float32)[:, None], colsum.shape)]
    )
    for bit in (1, 2, 4):
        sums = sums + swap(sums, "row", bit)
    colsum = sums[:blocks_here]
    counts = sums[blocks_here:, :1] * float(panel_rows)
    scale_second = weight_second * counts / jnp.where(counts > 0, colsum, 1.0)
    all_second = jnp.concatenate(four(scale_second, 1, 1, True))
    all_second = jnp.concatenate(four(all_second, 4, 1, True))
    lines = ((named // blocks_here) ^ column) * blocks_here + named % blocks_here

    chosen = select(ids, place, back.reshape(block_count, chunk, half), product.shape)
    home = lax.all_to_all(chosen, "col", split_axis=0, concat_axis=0, tiled=True)
    new_plan = final_scale(lines, home, scale_first[:, None], all_second, 4)
    return (new_plan, scale_first, scale_second)


def solution(mesh):
    return jax.shard_map(
        local,
        mesh=mesh,
        in_specs=(
            P("row", "col", "pan"),
            P("row", "col"),
            P("row", None, None, None),
            P("row", None),
            P("col", None, None, "pan"),
            P("col", None),
            P("row"),
            P("col", "pan"),
            P("row"),
            P("col", "pan"),
        ),
        out_specs=(P("row", "col", "pan"), P("row"), P("col", "pan")),
        check_vma=False,
    )
```

time: 443 us -> 183 us (0.41)
  blocking collectives: 178 us -> 31.2 us
  waiting for transfers between devices: 137 us -> 38.7 us
  starting transfers between devices: 14.5 us -> 77.7 us
  matrix products: 47.4 us -> 0 us
  local copies, waits for them, and re-layouts: 40.8 us -> 8.48 us
  Pallas kernels: 0 us -> 24.4 us
  between operations: 14.3 us -> 0.9 us
  other arithmetic: 10 us -> 1 us
    all_to_all x2 -> x3, waiting for transfers between devices: 121 us -> 12 us  [the longest x1 8.12 us: local(): lax.all_to_all(kernel, 'col', split_axis=0, concat_axis=0, tiled=True)]
    psum x2 -> x0, blocking collectives: 83.9 us -> none  [the longest x1 67.6 us: local(): row_totals = lax.psum(jnp.sum(kernel_values, axis=(1, 2)), ('col', 'pan'))]
    ppermute x0 -> x27, starting transfers between devices: none -> 62.7 us  [the longest x22 52.9 us: step_row(): return lax.ppermute(value, ('row', 'col'), pairs)]
    all_to_all x1, blocking collectives: 93.6 us -> 31.2 us  [local(): lax.all_to_all(merged, 'col', split_axis=0, concat_axis=0, tiled=True)]
    dot_general x9 -> x0, matrix products: 47.4 us -> none  [the longest x1 10.1 us: second_product(): jnp.einsum('rkb,kblh->rlh', dense_plan, panel_matrix, preferred_element_t...]
    ppermute x0 -> x27, waiting for transfers between devices: none -> 26.7 us  [the longest x22 19 us: step_row(): return lax.ppermute(value, ('row', 'col'), pairs)]
    pallas_call x0 -> x8, Pallas kernels: none -> 24.4 us  [the longest x1 7.42 us: first_product(): pl.pallas_call(first_kernel, grid_spec=pltpu.PrefetchScalarGridSpec(num_s...]
    all_gather x1 -> x0, waiting for transfers between devices: 15.7 us -> none  [local(): gathered = lax.all_gather(dense_plan, 'pan', axis=2, tiled=True)]
  transfers between devices with their start and end apart: 3 -> 30, of which waited for: 2 -> 16; matrix products, arithmetic and copies ran while one was open for 11% -> 1% of each run, Pallas kernels for 0% -> 3%
where the time goes in v1:
time: 183 us; the launch traced here: 182 us
  starting transfers between devices  77.7 us (42%)
  waiting for transfers between devices  38.7 us (21%)
  blocking collectives  31.2 us (17%)
  Pallas kernels  24.4 us (13%)
  local copies, waits for them, and re-layouts  8.48 us (5%)
    ppermute x22, starting transfers between devices, step_row(): return lax.ppermute(value, ('row', 'col'), pairs)  52.9 us
    all_to_all x1, blocking collectives, local(): lax.all_to_all(merged, 'col', split_axis=0, concat_axis=0, tiled=True)  31.2 us
    ppermute x22, waiting for transfers between devices, step_row(): return lax.ppermute(value, ('row', 'col'), pairs)  19 us
    ppermute x5, starting transfers between devices, swap(): return lax.ppermute(value, axis, [(i, i ^ bit) for i in range(size)])  9.8 us
    all_to_all x1, waiting for transfers between devices, local(): lax.all_to_all(kernel, 'col', split_axis=0, concat_axis=0, tiled=True)  8.12 us
    unnamed x33, local copies, waits for them, and re-layouts  7.87 us
    ppermute x5, waiting for transfers between devices, swap(): return lax.ppermute(value, axis, [(i, i ^ bit) for i in range(size)])  7.69 us
    pallas_call x1, Pallas kernels, first_product(): pl.pallas_call(first_kernel, grid_spec=pltpu.PrefetchScalarGridSpec(num_s...  7.42 us
  transfers between devices with their start and end apart: 30, of which 16 were waited for; matrix products, arithmetic and copies ran while one was open for 1% of the time, Pallas kernels for 3%

profile of v1, /device:TPU:32, one launch (start us, length us, event | category | flops | bytes accessed | tf_op | source)
XLA Modules:
  0.0 182.3 jit_solution(12844316683731660338)
XLA Ops:
  0.6 7.4 %first_product.1 = bf16[16,8,64,128]{3,2,1,0:T(8,128)(2,1)} custom-call(s32[4,3]{1,0:T(4,128)} %near.3, bf16[1024,8,128]{2,1,0:T(8,128)(2,1)} %x_ref.1, bf16[4,3,256,256]{3,2,1,0:T(8,128)(2,1)} %c_ref.1), custom_call_target="tpu_custom_call" | custom-call | flops 1610612736 | bytes 6291456 | tf_op jit(solution)/shard_map/first_product/pallas_call | solution.py:57
  8.1 7.2 %all-to-all-start = ((bf16[16,8,64,128]{3,2,1,0:T(8,128)(2,1)}), bf16[16,8,64,128]{3,2,1,0:T(8,128)(2,1)S(1)}, u32[]{:S(2)}, u32[]{:S(2)}) async-start(bf16[16,8,64,128]{3,2,1,0:T(8,128)(2,1)} %first_product.1), calls=%async_computation | async-start | bytes 4194304 | tf_op jit(solution)/shard_map/all_to_all | solution.py:347
  15.2 2.0 %collective-permute-start = (s32[8]{0:T(128)S(1)}, s32[8]{0:T(128)S(1)}, u32[]{:S(2)}, u32[]{:S(2)}) collective-permute-start(s32[8]{0:T(128)S(1)} %bitcast.20), channel_id=1, source_target_pairs={{0,32},{2,34},{4,36},{6,38},{8,40},{10,42},{12,44},{14,46},{16,48}... | collective-permute-start | bytes 104 | tf_op jit(solution)/shard_map/ppermute | solution.py:314
  17.2 3.3 %collective-permute-start.1 = (s32[8]{0:T(128)S(1)}, s32[8]{0:T(128)S(1)}, u32[]{:S(2)}, u32[]{:S(2)}) collective-permute-start(s32[8]{0:T(128)S(1)} %bitcast.21), channel_id=1, source_target_pairs={{0,34},{2,32},{4,38},{6,36},{8,42},{10,40},{12,46},{14,44},{16,50}... | collective-permute-start | bytes 104 | tf_op jit(solution)/shard_map/ppermute | solution.py:314
  20.5 5.2 %collective-permute-start.2 = (s32[8]{0:T(128)S(1)}, s32[8]{0:T(128)S(1)}, u32[]{:S(2)}, u32[]{:S(2)}) collective-permute-start(s32[8]{0:T(128)S(1)} %bitcast.22), channel_id=1, source_target_pairs={{0,36},{2,38},{4,32},{6,34},{8,44},{10,46},{12,40},{14,42},{16,52}... | collective-permute-start | bytes 104 | tf_op jit(solution)/shard_map/ppermute | solution.py:314
  26.3 1.9 %copy-done.1 = bf16[8,6,256,128]{3,2,1,0:T(8,128)(2,1)S(1)} copy-done((bf16[8,6,256,128]{3,2,1,0:T(8,128)(2,1)S(1)}, bf16[8,6,256,128]{3,2,1,0:T(8,128)(2,1)}, u32[]{:S(2)}) %copy-start.1) | copy-done | bytes 3145752
  28.2 1.6 panel_matrix.1
  29.9 1.4 copy-done.2
  31.2 1.4 copy-done.4
  33.7 1.5 collective-permute-start.5
  35.2 2.2 %collective-permute-start.6 = (s32[32]{0:T(128)S(1)}, s32[32]{0:T(128)S(1)}, u32[]{:S(2)}, u32[]{:S(2)}) collective-permute-start(s32[32]{0:T(128)S(1)} %pad_add_fusion), channel_id=1, source_target_pairs={{0,240},{2,242},{4,244},{6,246},{8,248},{10,250},{12,252},{14,254}... | collective-permute-start | bytes 392 | tf_op jit(solution)/shard_map/ppermute | solution.py:314
  38.4 1.3 collective-permute-done.5
  39.7 1.5 collective-permute-done.6
  41.2 1.9 %collective-permute-done.7 = s32[32]{0:T(128)S(1)} collective-permute-done((s32[32]{0:T(128)S(1)}, s32[32]{0:T(128)S(1)}, u32[]{:S(2)}, u32[]{:S(2)}) %collective-permute-start.7) | collective-permute-done | bytes 160 | tf_op jit(solution)/shard_map/ppermute | solution.py:314
  43.2 3.9 %all-to-all-done.x_ref = bf16[16,8,64,128]{3,2,1,0:T(8,128)(2,1)S(1)} async-done(((bf16[16,8,64,128]{3,2,1,0:T(8,128)(2,1)}), bf16[16,8,64,128]{3,2,1,0:T(8,128)(2,1)S(1)}, u32[]{:S(2)}, u32[]{:S(2)}) %all-to-all-start) | async-done | bytes 2097184 | tf_op jit(solution)/shard_map/all_to_all | solution.py:347
  47.0 1.6 merge.1
  48.7 31.2 %all_to_all.20.x_ref = bf16[16,8,64,128]{3,2,1,0:T(8,128)(2,1)S(1)} all-to-all(bf16[16,8,64,128]{3,2,1,0:T(8,128)(2,1)S(1)} %bitcast.14), channel_id=1, replica_groups=mesh['row'=8,'col'=16,'pan'=2] {'col'}, dimensions={0} | all-to-all | bytes 4194304 | tf_op jit(solution)/shard_map/all_to_all | solution.py:356
  80.4 1.6 copy-done.5
  82.0 2.6 %second_near.1.near_ref = f32[1024,1024]{1,0:T(8,128)S(1)} custom-call(bf16[16,8,64,128]{3,2,1,0:T(8,128)(2,1)S(1)} %all_to_all.20.x_ref, bf16[1024,1024]{1,0:T(8,128)(2,1)S(1)} %copy-done.5), custom_call_target="tpu_custom_call" | custom-call | flops 2147483648 | bytes 8388608 | tf_op jit(solution)/shard_map/second_near/pallas_call | solution.py:177
  84.5 5.5 %second_far.1 = (bf16[16,8,64,128]{3,2,1,0:T(8,128)(2,1)}, f32[2,1,512]{2,1,0:T(1,128)S(1)}) custom-call(bf16[16,8,64,128]{3,2,1,0:T(8,128)(2,1)} %collective-permute-done.8.x_ref, bf16[1024,1024]{1,0:T(8,128)(2,1)S(1)} %copy-done.3, f32[1024,1024]{1,0:T(8,128)S(1)} %second_near.1.near_ref, f32[1024,1]{1,0:T(8,128)S(1)} %copy.15.first_ref, ...), custom_call_target="tpu_custom_call" | custom-call | flops 2147483648 | bytes 10485760 | tf_op jit(solution)/shard_map/second_far/pallas_call | solution.py:217
  90.1 3.9 %all-to-all-start.2 = ((bf16[16,8,64,128]{3,2,1,0:T(8,128)(2,1)}), bf16[16,8,64,128]{3,2,1,0:T(8,128)(2,1)S(1)}, u32[]{:S(2)}, u32[]{:S(2)}) async-start(bf16[16,8,64,128]{3,2,1,0:T(8,128)(2,1)} %get-tuple-element.15.x_ref), calls=%async_computation.2 | async-start | bytes 4194304 | tf_op jit(solution)/shard_map/all_to_all | solution.py:361
  95.3 1.9 %collective-permute-start.10 = (f32[8,128]{1,0:T(8,128)S(1)}, f32[8,128]{1,0:T(8,128)S(1)}, u32[]{:S(2)}, u32[]{:S(2)}) collective-permute-start(f32[8,128]{1,0:T(8,128)S(1)} %add.54), channel_id=1, source_target_pairs={{0,32},{2,34},{4,36},{6,38},{8,40},{10,42},{12,44},{14,46},{16,48}... | collective-permute-start | bytes 12296 | tf_op jit(solution)/shard_map/ppermute | solution.py:314
  97.3 2.9 %collective-permute-start.11 = (f32[8,128]{1,0:T(8,128)S(1)}, f32[8,128]{1,0:T(8,128)S(1)}, u32[]{:S(2)}, u32[]{:S(2)}) collective-permute-start(f32[8,128]{1,0:T(8,128)S(1)} %add.54), channel_id=1, source_target_pairs={{0,34},{2,32},{4,38},{6,36},{8,42},{10,40},{12,46},{14,44},{16,50}... | collective-permute-start | bytes 12296 | tf_op jit(solution)/shard_map/ppermute | solution.py:314
  100.2 5.2 %collective-permute-start.12 = (f32[8,128]{1,0:T(8,128)S(1)}, f32[8,128]{1,0:T(8,128)S(1)}, u32[]{:S(2)}, u32[]{:S(2)}) collective-permute-start(f32[8,128]{1,0:T(8,128)S(1)} %add.54), channel_id=1, source_target_pairs={{0,36},{2,38},{4,32},{6,34},{8,44},{10,46},{12,40},{14,42},{16,52}... | collective-permute-start | bytes 12296 | tf_op jit(solution)/shard_map/ppermute | solution.py:314
  106.7 4.4 %collective-permute-done.13 = f32[8,128]{1,0:T(8,128)S(1)} collective-permute-done((f32[8,128]{1,0:T(8,128)S(1)}, f32[8,128]{1,0:T(8,128)S(1)}, u32[]{:S(2)}, u32[]{:S(2)}) %collective-permute-start.13) | collective-permute-done | bytes 4128 | tf_op jit(solution)/shard_map/ppermute | solution.py:314
  111.3 1.1 collective-permute-start.15
  112.4 2.5 %collective-permute-start.16 = (f32[8,128]{1,0:T(8,128)S(1)}, f32[8,128]{1,0:T(8,128)S(1)}, u32[]{:S(2)}, u32[]{:S(2)}) collective-permute-start(f32[8,128]{1,0:T(8,128)S(1)} %add_add_fusion), channel_id=1, source_target_pairs={{0,240},{2,242},{4,244},{6,246},{8,248},{10,250},{12,252},{14,254}... | collective-permute-start | bytes 12296 | tf_op jit(solution)/shard_map/ppermute | solution.py:314
  114.8 2.5 %collective-permute-start.17 = (f32[8,128]{1,0:T(8,128)S(1)}, f32[8,128]{1,0:T(8,128)S(1)}, u32[]{:S(2)}, u32[]{:S(2)}) collective-permute-start(f32[8,128]{1,0:T(8,128)S(1)} %add_add_fusion), channel_id=1, source_target_pairs={{0,248},{2,250},{4,252},{6,254},{8,240},{10,242},{12,244},{14,246}... | collective-permute-start | bytes 12296 | tf_op jit(solution)/shard_map/ppermute | solution.py:314
  117.5 1.6 collective-permute-done.16
  119.1 1.4 collective-permute-done.17
  120.6 8.1 %all-to-all-done.2 = bf16[16,8,64,128]{3,2,1,0:T(8,128)(2,1)S(1)} async-done(((bf16[16,8,64,128]{3,2,1,0:T(8,128)(2,1)}), bf16[16,8,64,128]{3,2,1,0:T(8,128)(2,1)S(1)}, u32[]{:S(2)}, u32[]{:S(2)}) %all-to-all-start.2) | async-done | bytes 2097184 | tf_op jit(solution)/shard_map/all_to_all | solution.py:361
  128.7 2.0 %select.7 = bf16[16,8,64,128]{3,2,1,0:T(8,128)(2,1)} custom-call(s32[128]{0:T(128)S(1)} %pad_add_fusion.1.ids, s32[1]{0:T(128)} %bitcast.2.place, bf16[128,64,128]{2,1,0:T(8,128)(2,1)S(1)} %bitcast.13), custom_call_target="tpu_custom_call" | custom-call | bytes 4194304 | tf_op jit(solution)/shard_map/select/pallas_call | solution.py:145
  130.8 4.0 %all-to-all-start.3 = ((bf16[16,8,64,128]{3,2,1,0:T(8,128)(2,1)}), bf16[16,8,64,128]{3,2,1,0:T(8,128)(2,1)S(1)}, u32[]{:S(2)}, u32[]{:S(2)}) async-start(bf16[16,8,64,128]{3,2,1,0:T(8,128)(2,1)} %select.7), calls=%async_computation.3 | async-start | bytes 4194304 | tf_op jit(solution)/shard_map/all_to_all | solution.py:383
  134.9 1.6 copy-done
  137.0 3.6 %collective-permute-done.18 = f32[16,128]{1,0:T(8,128)S(1)} collective-permute-done((f32[16,128]{1,0:T(8,128)S(1)}, f32[16,128]{1,0:T(8,128)S(1)}, u32[]{:S(2)}, u32[]{:S(2)}) %collective-permute-start.18) | collective-permute-done | bytes 8224 | tf_op jit(solution)/shard_map/ppermute | solution.py:304
  140.7 3.2 %collective-permute-start.19 = (f32[16,128]{1,0:T(8,128)S(1)}, f32[16,128]{1,0:T(8,128)S(1)}, u32[]{:S(2)}, u32[]{:S(2)}) collective-permute-start(f32[16,128]{1,0:T(8,128)S(1)} %fusion.4), channel_id=1, source_target_pairs={{0,64},{32,96},{64,0},{96,32},{128,192},{160,224},{192,128},{224,1... | collective-permute-start | bytes 24584 | tf_op jit(solution)/shard_map/ppermute | solution.py:304
  143.8 1.6 collective-permute-done.19
  145.5 6.0 %collective-permute-start.20 = (f32[16,128]{1,0:T(8,128)S(1)}, f32[16,128]{1,0:T(8,128)S(1)}, u32[]{:S(2)}, u32[]{:S(2)}) collective-permute-start(f32[16,128]{1,0:T(8,128)S(1)} %add.62), channel_id=1, source_target_pairs={{0,128},{32,160},{64,192},{96,224},{128,0},{160,32},{192,64},{224,... | collective-permute-start | bytes 24584 | tf_op jit(solution)/shard_map/ppermute | solution.py:304
  151.4 1.6 collective-permute-done.20
  153.4 3.0 %collective-permute-start.21 = (f32[8,128]{1,0:T(8,128)S(1)}, f32[8,128]{1,0:T(8,128)S(1)}, u32[]{:S(2)}, u32[]{:S(2)}) collective-permute-start(f32[8,128]{1,0:T(8,128)S(1)} %get-tuple-element.18), channel_id=1, source_target_pairs={{0,34},{2,32},{4,38},{6,36},{8,42},{10,40},{12,46},{14,44},{16,50}... | collective-permute-start | bytes 12296 | tf_op jit(solution)/shard_map/ppermute | solution.py:314
  156.4 4.0 %collective-permute-start.22 = (f32[8,128]{1,0:T(8,128)S(1)}, f32[8,128]{1,0:T(8,128)S(1)}, u32[]{:S(2)}, u32[]{:S(2)}) collective-permute-start(f32[8,128]{1,0:T(8,128)S(1)} %get-tuple-element.18), channel_id=1, source_target_pairs={{0,36},{2,38},{4,32},{6,34},{8,44},{10,46},{12,40},{14,42},{16,52}... | collective-permute-start | bytes 12296 | tf_op jit(solution)/shard_map/ppermute | solution.py:314
  160.3 2.7 %collective-permute-start.23 = (f32[8,128]{1,0:T(8,128)S(1)}, f32[8,128]{1,0:T(8,128)S(1)}, u32[]{:S(2)}, u32[]{:S(2)}) collective-permute-start(f32[8,128]{1,0:T(8,128)S(1)} %get-tuple-element.18), channel_id=1, source_target_pairs={{0,38},{2,36},{4,34},{6,32},{8,46},{10,44},{12,42},{14,40},{16,54}... | collective-permute-start | bytes 12296 | tf_op jit(solution)/shard_map/ppermute | solution.py:314
  163.3 2.8 %collective-permute-done.23 = f32[8,128]{1,0:T(8,128)S(1)} collective-permute-done((f32[8,128]{1,0:T(8,128)S(1)}, f32[8,128]{1,0:T(8,128)S(1)}, u32[]{:S(2)}, u32[]{:S(2)}) %collective-permute-start.23) | collective-permute-done | bytes 4128 | tf_op jit(solution)/shard_map/ppermute | solution.py:314
  166.1 4.0 %collective-permute-start.24 = (f32[32,128]{1,0:T(8,128)S(1)}, f32[32,128]{1,0:T(8,128)S(1)}, u32[]{:S(2)}, u32[]{:S(2)}) collective-permute-start(f32[32,128]{1,0:T(8,128)S(1)} %pad_maximum_fusion), channel_id=1, source_target_pairs={{0,40},{2,42},{4,44},{6,46},{8,32},{10,34},{12,36},{14,38},{16,56}... | collective-permute-start | bytes 49160 | tf_op jit(solution)/shard_map/ppermute | solution.py:314
  170.1 3.1 %collective-permute-start.25 = (f32[32,128]{1,0:T(8,128)S(1)}, f32[32,128]{1,0:T(8,128)S(1)}, u32[]{:S(2)}, u32[]{:S(2)}) collective-permute-start(f32[32,128]{1,0:T(8,128)S(1)} %pad_maximum_fusion), channel_id=1, source_target_pairs={{0,48},{2,50},{4,52},{6,54},{8,56},{10,58},{12,60},{14,62},{16,32}... | collective-permute-start | bytes 49160 | tf_op jit(solution)/shard_map/ppermute | solution.py:314
  173.2 2.2 %collective-permute-start.26 = (f32[32,128]{1,0:T(8,128)S(1)}, f32[32,128]{1,0:T(8,128)S(1)}, u32[]{:S(2)}, u32[]{:S(2)}) collective-permute-start(f32[32,128]{1,0:T(8,128)S(1)} %pad_maximum_fusion), channel_id=1, source_target_pairs={{0,56},{2,58},{4,60},{6,62},{8,48},{10,50},{12,52},{14,54},{16,40}... | collective-permute-start | bytes 49160 | tf_op jit(solution)/shard_map/ppermute | solution.py:314
  176.2 2.8 %collective-permute-done.26 = f32[32,128]{1,0:T(8,128)S(1)} collective-permute-done((f32[32,128]{1,0:T(8,128)S(1)}, f32[32,128]{1,0:T(8,128)S(1)}, u32[]{:S(2)}, u32[]{:S(2)}) %collective-permute-start.26) | collective-permute-done | bytes 16416 | tf_op jit(solution)/shard_map/ppermute | solution.py:314
  179.1 3.3 %final_scale.1 = bf16[1024,8,128]{2,1,0:T(8,128)(2,1)} custom-call(s32[8]{0:T(128)S(1)} %fusion.3.lines, bf16[16,8,64,128]{3,2,1,0:T(8,128)(2,1)S(1)} %all-to-all-done.3.x_ref, f32[1024,1]{1,0:T(8,128)S(1)} %copy.16.first_ref, f32[128,128]{1,0:T(8,128)S(1)} %constant_dynamic-update-slice_fusion.second_ref), custom_call_target="tpu_custom_call" | custom-call | bytes 5242880 | tf_op jit(solution)/shard_map/final_scale/pallas_call | solution.py:283
  (83 shorter events, 8.3 us)
Async XLA Ops:
  8.1 7.2 %copy-start.13 = (s32[1,8]{1,0:T(1,128)S(1)}, s32[1,8]{1,0:T(1,128)}, u32[]{:S(2)}) copy-start(s32[1,8]{1,0:T(1,128)} %param.11) | copy-start | bytes 100
  8.1 18.3 %copy-start.6 = (s32[8,6]{1,0:T(8,128)S(1)}, s32[8,6]{1,0:T(8,128)}, u32[]{:S(2)}) copy-start(s32[8,6]{1,0:T(8,128)} %near.2) | copy-start | bytes 580
  8.1 39.0 %all-to-all-start = ((bf16[16,8,64,128]{3,2,1,0:T(8,128)(2,1)}), bf16[16,8,64,128]{3,2,1,0:T(8,128)(2,1)S(1)}, u32[]{:S(2)}, u32[]{:S(2)}) async-start(bf16[16,8,64,128]{3,2,1,0:T(8,128)(2,1)} %first_product.1), calls=%async_computation | async-start | bytes 4194304 | tf_op jit(solution)/shard_map/all_to_all | solution.py:347
  15.2 17.4 %collective-permute-start = (s32[8]{0:T(128)S(1)}, s32[8]{0:T(128)S(1)}, u32[]{:S(2)}, u32[]{:S(2)}) collective-permute-start(s32[8]{0:T(128)S(1)} %bitcast.20), channel_id=1, source_target_pairs={{0,32},{2,34},{4,36},{6,38},{8,40},{10,42},{12,44},{14,46},{16,48}... | collective-permute-start | bytes 104 | tf_op jit(solution)/shard_map/ppermute | solution.py:314
  17.2 15.4 %collective-permute-start.1 = (s32[8]{0:T(128)S(1)}, s32[8]{0:T(128)S(1)}, u32[]{:S(2)}, u32[]{:S(2)}) collective-permute-start(s32[8]{0:T(128)S(1)} %bitcast.21), channel_id=1, source_target_pairs={{0,34},{2,32},{4,38},{6,36},{8,42},{10,40},{12,46},{14,44},{16,50}... | collective-permute-start | bytes 104 | tf_op jit(solution)/shard_map/ppermute | solution.py:314
  20.5 12.1 %collective-permute-start.2 = (s32[8]{0:T(128)S(1)}, s32[8]{0:T(128)S(1)}, u32[]{:S(2)}, u32[]{:S(2)}) collective-permute-start(s32[8]{0:T(128)S(1)} %bitcast.22), channel_id=1, source_target_pairs={{0,36},{2,38},{4,32},{6,34},{8,44},{10,46},{12,40},{14,42},{16,52}... | collective-permute-start | bytes 104 | tf_op jit(solution)/shard_map/ppermute | solution.py:314
  25.8 6.9 %collective-permute-start.3 = (s32[8]{0:T(128)S(1)}, s32[8]{0:T(128)S(1)}, u32[]{:S(2)}, u32[]{:S(2)}) collective-permute-start(s32[8]{0:T(128)S(1)} %bitcast.23), channel_id=1, source_target_pairs={{0,38},{2,36},{4,34},{6,32},{8,46},{10,44},{12,42},{14,40},{16,54}... | collective-permute-start | bytes 104 | tf_op jit(solution)/shard_map/ppermute | solution.py:314
  26.3 1.9 %copy-start.1 = (bf16[8,6,256,128]{3,2,1,0:T(8,128)(2,1)S(1)}, bf16[8,6,256,128]{3,2,1,0:T(8,128)(2,1)}, u32[]{:S(2)}) copy-start(bf16[8,6,256,128]{3,2,1,0:T(8,128)(2,1)} %v_ref.1) | copy-start | bytes 9437188
  29.9 1.4 copy-start.2
  31.2 1.4 copy-start.4
  32.7 5.7 %collective-permute-start.4 = (s32[32]{0:T(128)S(1)}, s32[32]{0:T(128)S(1)}, u32[]{:S(2)}, u32[]{:S(2)}) collective-permute-start(s32[32]{0:T(128)S(1)} %pad_add_fusion), channel_id=1, source_target_pairs={{0,224},{2,226},{4,228},{6,230},{8,232},{10,234},{12,236},{14,238}... | collective-permute-start | bytes 392 | tf_op jit(solution)/shard_map/ppermute | solution.py:314
  33.7 5.9 %collective-permute-start.5 = (s32[32]{0:T(128)S(1)}, s32[32]{0:T(128)S(1)}, u32[]{:S(2)}, u32[]{:S(2)}) collective-permute-start(s32[32]{0:T(128)S(1)} %pad_add_fusion), channel_id=1, source_target_pairs={{0,232},{2,234},{4,236},{6,238},{8,224},{10,226},{12,228},{14,230}... | collective-permute-start | bytes 392 | tf_op jit(solution)/shard_map/ppermute | solution.py:314
  35.2 6.0 %collective-permute-start.6 = (s32[32]{0:T(128)S(1)}, s32[32]{0:T(128)S(1)}, u32[]{:S(2)}, u32[]{:S(2)}) collective-permute-start(s32[32]{0:T(128)S(1)} %pad_add_fusion), channel_id=1, source_target_pairs={{0,240},{2,242},{4,244},{6,246},{8,248},{10,250},{12,252},{14,254}... | collective-permute-start | bytes 392 | tf_op jit(solution)/shard_map/ppermute | solution.py:314
  37.4 5.7 %collective-permute-start.7 = (s32[32]{0:T(128)S(1)}, s32[32]{0:T(128)S(1)}, u32[]{:S(2)}, u32[]{:S(2)}) collective-permute-start(s32[32]{0:T(128)S(1)} %pad_add_fusion), channel_id=1, source_target_pairs={{0,248},{2,250},{4,252},{6,254},{8,240},{10,242},{12,244},{14,246}... | collective-permute-start | bytes 392 | tf_op jit(solution)/shard_map/ppermute | solution.py:314
  48.6 31.2 %copy-start.9 = (f32[1024]{0:T(1024)S(1)}, f32[1024]{0:T(1024)}, u32[]{:S(2)}) copy-start(f32[1024]{0:T(1024)} %param.18) | copy-start | bytes 12292
  48.7 31.6 %copy-start.11 = (f32[8,128]{1,0:T(8,128)S(1)}, f32[8,128]{1,0:T(8,128)}, u32[]{:S(2)}) copy-start(f32[8,128]{1,0:T(8,128)} %param.19) | copy-start | bytes 12292
  79.8 4.7 %collective-permute-start.8 = (bf16[16,8,64,128]{3,2,1,0:T(8,128)(2,1)S(1)}, bf16[16,8,64,128]{3,2,1,0:T(8,128)(2,1)}, u32[]{:S(2)}, u32[]{:S(2)}) collective-permute-start(bf16[16,8,64,128]{3,2,1,0:T(8,128)(2,1)S(1)} %all_to_all.20.x_ref), channel_id=1, source_target_pairs={{0,1},{1,0},{2,3},{3,2},{4,5},{5,4},{6,7},{7,6},{8,9},{9,8},{10,11... | collective-permute-start | bytes 6291464 | tf_op jit(solution)/shard_map/ppermute | solution.py:304
  80.4 1.6 copy-start.5
  82.0 2.6 %copy-start.3 = (bf16[1024,1024]{1,0:T(8,128)(2,1)S(1)}, bf16[1024,1024]{1,0:T(8,128)(2,1)}, u32[]{:S(2)}) copy-start(bf16[1024,1024]{1,0:T(8,128)(2,1)} %copy-done.2) | copy-start | bytes 6291460
  90.1 30.5 %copy-start.12 = (f32[1024]{0:T(1024)S(1)}, f32[1024]{0:T(1024)}, u32[]{:S(2)}) copy-start(f32[1024]{0:T(1024)} %param.16) | copy-start | bytes 12292
  90.1 38.7 %all-to-all-start.2 = ((bf16[16,8,64,128]{3,2,1,0:T(8,128)(2,1)}), bf16[16,8,64,128]{3,2,1,0:T(8,128)(2,1)S(1)}, u32[]{:S(2)}, u32[]{:S(2)}) async-start(bf16[16,8,64,128]{3,2,1,0:T(8,128)(2,1)} %get-tuple-element.15.x_ref), calls=%async_computation.2 | async-start | bytes 4194304 | tf_op jit(solution)/shard_map/all_to_all | solution.py:361
  93.9 1.4 collective-permute-start.9
  95.3 11.0 %collective-permute-start.10 = (f32[8,128]{1,0:T(8,128)S(1)}, f32[8,128]{1,0:T(8,128)S(1)}, u32[]{:S(2)}, u32[]{:S(2)}) collective-permute-start(f32[8,128]{1,0:T(8,128)S(1)} %add.54), channel_id=1, source_target_pairs={{0,32},{2,34},{4,36},{6,38},{8,40},{10,42},{12,44},{14,46},{16,48}... | collective-permute-start | bytes 12296 | tf_op jit(solution)/shard_map/ppermute | solution.py:314
  97.3 9.1 %collective-permute-start.11 = (f32[8,128]{1,0:T(8,128)S(1)}, f32[8,128]{1,0:T(8,128)S(1)}, u32[]{:S(2)}, u32[]{:S(2)}) collective-permute-start(f32[8,128]{1,0:T(8,128)S(1)} %add.54), channel_id=1, source_target_pairs={{0,34},{2,32},{4,38},{6,36},{8,42},{10,40},{12,46},{14,44},{16,50}... | collective-permute-start | bytes 12296 | tf_op jit(solution)/shard_map/ppermute | solution.py:314
  100.2 6.6 %collective-permute-start.12 = (f32[8,128]{1,0:T(8,128)S(1)}, f32[8,128]{1,0:T(8,128)S(1)}, u32[]{:S(2)}, u32[]{:S(2)}) collective-permute-start(f32[8,128]{1,0:T(8,128)S(1)} %add.54), channel_id=1, source_target_pairs={{0,36},{2,38},{4,32},{6,34},{8,44},{10,46},{12,40},{14,42},{16,52}... | collective-permute-start | bytes 12296 | tf_op jit(solution)/shard_map/ppermute | solution.py:314
  105.4 5.8 %collective-permute-start.13 = (f32[8,128]{1,0:T(8,128)S(1)}, f32[8,128]{1,0:T(8,128)S(1)}, u32[]{:S(2)}, u32[]{:S(2)}) collective-permute-start(f32[8,128]{1,0:T(8,128)S(1)} %add.54), channel_id=1, source_target_pairs={{0,38},{2,36},{4,34},{6,32},{8,46},{10,44},{12,42},{14,40},{16,54}... | collective-permute-start | bytes 12296 | tf_op jit(solution)/shard_map/ppermute | solution.py:314
  111.2 6.3 %collective-permute-start.14 = (f32[8,128]{1,0:T(8,128)S(1)}, f32[8,128]{1,0:T(8,128)S(1)}, u32[]{:S(2)}, u32[]{:S(2)}) collective-permute-start(f32[8,128]{1,0:T(8,128)S(1)} %add_add_fusion), channel_id=1, source_target_pairs={{0,224},{2,226},{4,228},{6,230},{8,232},{10,234},{12,236},{14,238}... | collective-permute-start | bytes 12296 | tf_op jit(solution)/shard_map/ppermute | solution.py:314
  111.3 6.2 %collective-permute-start.15 = (f32[8,128]{1,0:T(8,128)S(1)}, f32[8,128]{1,0:T(8,128)S(1)}, u32[]{:S(2)}, u32[]{:S(2)}) collective-permute-start(f32[8,128]{1,0:T(8,128)S(1)} %add_add_fusion), channel_id=1, source_target_pairs={{0,232},{2,234},{4,236},{6,238},{8,224},{10,226},{12,228},{14,230}... | collective-permute-start | bytes 12296 | tf_op jit(solution)/shard_map/ppermute | solution.py:314
  112.4 6.7 %collective-permute-start.16 = (f32[8,128]{1,0:T(8,128)S(1)}, f32[8,128]{1,0:T(8,128)S(1)}, u32[]{:S(2)}, u32[]{:S(2)}) collective-permute-start(f32[8,128]{1,0:T(8,128)S(1)} %add_add_fusion), channel_id=1, source_target_pairs={{0,240},{2,242},{4,244},{6,246},{8,248},{10,250},{12,252},{14,254}... | collective-permute-start | bytes 12296 | tf_op jit(solution)/shard_map/ppermute | solution.py:314
  114.8 5.7 %collective-permute-start.17 = (f32[8,128]{1,0:T(8,128)S(1)}, f32[8,128]{1,0:T(8,128)S(1)}, u32[]{:S(2)}, u32[]{:S(2)}) collective-permute-start(f32[8,128]{1,0:T(8,128)S(1)} %add_add_fusion), channel_id=1, source_target_pairs={{0,248},{2,250},{4,252},{6,254},{8,240},{10,242},{12,244},{14,246}... | collective-permute-start | bytes 12296 | tf_op jit(solution)/shard_map/ppermute | solution.py:314
  120.6 42.5 %copy-start.7 = (f32[1024]{0:T(1024)}, f32[1024]{0:T(1024)S(1)}, u32[]{:S(2)}) copy-start(f32[1024]{0:T(1024)S(1)} %get-tuple-element.20) | copy-start | bytes 12292
  130.8 48.3 %all-to-all-start.3 = ((bf16[16,8,64,128]{3,2,1,0:T(8,128)(2,1)}), bf16[16,8,64,128]{3,2,1,0:T(8,128)(2,1)S(1)}, u32[]{:S(2)}, u32[]{:S(2)}) async-start(bf16[16,8,64,128]{3,2,1,0:T(8,128)(2,1)} %select.7), calls=%async_computation.3 | async-start | bytes 4194304 | tf_op jit(solution)/shard_map/all_to_all | solution.py:383
  134.8 18.5 %copy-start.10 = (f32[8,128]{1,0:T(8,128)S(1)}, f32[8,128]{1,0:T(8,128)}, u32[]{:S(2)}) copy-start(f32[8,128]{1,0:T(8,128)} %param.17) | copy-start | bytes 12292
  134.9 1.6 copy-start
  136.9 3.7 %collective-permute-start.18 = (f32[16,128]{1,0:T(8,128)S(1)}, f32[16,128]{1,0:T(8,128)S(1)}, u32[]{:S(2)}, u32[]{:S(2)}) collective-permute-start(f32[16,128]{1,0:T(8,128)S(1)} %pad_maximum_fusion.1), channel_id=1, source_target_pairs={{0,32},{32,0},{64,96},{96,64},{128,160},{160,128},{192,224},{224,1... | collective-permute-start | bytes 24584 | tf_op jit(solution)/shard_map/ppermute | solution.py:304
  140.7 4.8 %collective-permute-start.19 = (f32[16,128]{1,0:T(8,128)S(1)}, f32[16,128]{1,0:T(8,128)S(1)}, u32[]{:S(2)}, u32[]{:S(2)}) collective-permute-start(f32[16,128]{1,0:T(8,128)S(1)} %fusion.4), channel_id=1, source_target_pairs={{0,64},{32,96},{64,0},{96,32},{128,192},{160,224},{192,128},{224,1... | collective-permute-start | bytes 24584 | tf_op jit(solution)/shard_map/ppermute | solution.py:304
  145.5 7.6 %collective-permute-start.20 = (f32[16,128]{1,0:T(8,128)S(1)}, f32[16,128]{1,0:T(8,128)S(1)}, u32[]{:S(2)}, u32[]{:S(2)}) collective-permute-start(f32[16,128]{1,0:T(8,128)S(1)} %add.62), channel_id=1, source_target_pairs={{0,128},{32,160},{64,192},{96,224},{128,0},{160,32},{192,64},{224,... | collective-permute-start | bytes 24584 | tf_op jit(solution)/shard_map/ppermute | solution.py:304
  153.4 29.0 %copy-start.8 = (f32[8,128]{1,0:T(8,128)}, f32[8,128]{1,0:T(8,128)S(1)}, u32[]{:S(2)}) copy-start(f32[8,128]{1,0:T(8,128)S(1)} %get-tuple-element.18) | copy-start | bytes 12292
  153.4 9.9 %collective-permute-start.21 = (f32[8,128]{1,0:T(8,128)S(1)}, f32[8,128]{1,0:T(8,128)S(1)}, u32[]{:S(2)}, u32[]{:S(2)}) collective-permute-start(f32[8,128]{1,0:T(8,128)S(1)} %get-tuple-element.18), channel_id=1, source_target_pairs={{0,34},{2,32},{4,38},{6,36},{8,42},{10,40},{12,46},{14,44},{16,50}... | collective-permute-start | bytes 12296 | tf_op jit(solution)/shard_map/ppermute | solution.py:314
  156.4 6.9 %collective-permute-start.22 = (f32[8,128]{1,0:T(8,128)S(1)}, f32[8,128]{1,0:T(8,128)S(1)}, u32[]{:S(2)}, u32[]{:S(2)}) collective-permute-start(f32[8,128]{1,0:T(8,128)S(1)} %get-tuple-element.18), channel_id=1, source_target_pairs={{0,36},{2,38},{4,32},{6,34},{8,44},{10,46},{12,40},{14,42},{16,52}... | collective-permute-start | bytes 12296 | tf_op jit(solution)/shard_map/ppermute | solution.py:314
  160.3 5.7 %collective-permute-start.23 = (f32[8,128]{1,0:T(8,128)S(1)}, f32[8,128]{1,0:T(8,128)S(1)}, u32[]{:S(2)}, u32[]{:S(2)}) collective-permute-start(f32[8,128]{1,0:T(8,128)S(1)} %get-tuple-element.18), channel_id=1, source_target_pairs={{0,38},{2,36},{4,34},{6,32},{8,46},{10,44},{12,42},{14,40},{16,54}... | collective-permute-start | bytes 12296 | tf_op jit(solution)/shard_map/ppermute | solution.py:314
  166.1 9.4 %collective-permute-start.24 = (f32[32,128]{1,0:T(8,128)S(1)}, f32[32,128]{1,0:T(8,128)S(1)}, u32[]{:S(2)}, u32[]{:S(2)}) collective-permute-start(f32[32,128]{1,0:T(8,128)S(1)} %pad_maximum_fusion), channel_id=1, source_target_pairs={{0,40},{2,42},{4,44},{6,46},{8,32},{10,34},{12,36},{14,38},{16,56}... | collective-permute-start | bytes 49160 | tf_op jit(solution)/shard_map/ppermute | solution.py:314
  170.1 6.1 %collective-permute-start.25 = (f32[32,128]{1,0:T(8,128)S(1)}, f32[32,128]{1,0:T(8,128)S(1)}, u32[]{:S(2)}, u32[]{:S(2)}) collective-permute-start(f32[32,128]{1,0:T(8,128)S(1)} %pad_maximum_fusion), channel_id=1, source_target_pairs={{0,48},{2,50},{4,52},{6,54},{8,56},{10,58},{12,60},{14,62},{16,32}... | collective-permute-start | bytes 49160 | tf_op jit(solution)/shard_map/ppermute | solution.py:314
  173.2 5.8 %collective-permute-start.26 = (f32[32,128]{1,0:T(8,128)S(1)}, f32[32,128]{1,0:T(8,128)S(1)}, u32[]{:S(2)}, u32[]{:S(2)}) collective-permute-start(f32[32,128]{1,0:T(8,128)S(1)} %pad_maximum_fusion), channel_id=1, source_target_pairs={{0,56},{2,58},{4,60},{6,62},{8,48},{10,50},{12,52},{14,54},{16,40}... | collective-permute-start | bytes 49160 | tf_op jit(solution)/shard_map/ppermute | solution.py:314

commit v2 on v0

v2 whole, which is shorter than its diff:
```python
import functools
import jax
import jax.numpy as jnp
from jax import lax
from jax.experimental import pallas as pl
from jax.experimental.pallas import tpu as pltpu
from jax.sharding import PartitionSpec as P

LARGEST = float(jnp.finfo(jnp.bfloat16).max)


def params(mebibytes=40):
    return pltpu.CompilerParams(
        dimension_semantics=("arbitrary",), vmem_limit_bytes=mebibytes << 20
    )


def cost(flops, moved):
    return pl.CostEstimate(flops=flops, bytes_accessed=moved, transcendentals=0)


VMEM = pl.BlockSpec(memory_space=pltpu.VMEM)
SMEM = pl.BlockSpec(memory_space=pltpu.SMEM)
ANY = pl.BlockSpec(memory_space=pl.ANY)


def first_kernel(near, named, x_hbm, c_hbm, o_hbm, x, c, flat, out, x_sem, c_sem, o_sem):
    tiles, count, rows, _ = c.shape
    slots, half = x.shape[1:]
    chunk = x.shape[0] // out.shape[0]
    parts = rows // chunk

    def load_x(tile):
        part = pl.ds(tile * rows, rows)
        return pltpu.make_async_copy(x_hbm.at[part], x.at[part], x_sem.at[tile])

    def load_c(tile):
        return pltpu.make_async_copy(c_hbm.at[tile], c.at[tile], c_sem.at[tile])

    def store(tile):
        part = pl.ds(tile * parts, parts)
        return pltpu.make_async_copy(out.at[part], o_hbm.at[part], o_sem.at[tile])

    for tile in range(tiles):
        load_x(tile).start()
    for tile in range(tiles):
        load_c(tile).start()
    lanes = lax.broadcasted_iota(jnp.int32, (8, half), 1)
    line = jnp.zeros((8, half), jnp.int32)
    for slot in range(slots):
        line = jnp.where(lanes == slot, named[slot], line)
    for part in range(out.shape[0]):
        out[part, slots * chunk :] = line.astype(jnp.float32).astype(jnp.bfloat16)
    for tile in range(tiles):
        load_x(tile).wait()
        flat[tile] = x[tile * rows : (tile + 1) * rows].reshape(rows, slots * half)
    for tile in range(tiles):
        load_c(tile).wait()
        total = None
        for q in range(count):
            term = jnp.dot(c[tile, q], flat[near[tile, q]], preferred_element_type=jnp.float32)
            total = term if total is None else total + term
        total = total.astype(jnp.bfloat16)
        for part in range(parts):
            for slot in range(slots):
                out[tile * parts + part, slot * chunk : (slot + 1) * chunk] = total[
                    part * chunk : (part + 1) * chunk, slot * half : (slot + 1) * half
                ]
        store(tile).start()
    for tile in range(tiles):
        store(tile).wait()


def first_product(x, values, near, named, col_count):
    panel_rows, slots, half = x.shape
    tiles, count, rows, _ = values.shape
    chunk = panel_rows // col_count
    shape = (col_count, slots * chunk + 8, half)
    return pl.pallas_call(
        first_kernel,
        in_specs=[SMEM, SMEM, ANY, ANY],
        out_specs=ANY,
        out_shape=pltpu.HBM(shape, jnp.bfloat16),
        scratch_shapes=[
            pltpu.VMEM(x.shape, jnp.bfloat16),
            pltpu.VMEM(values.shape, jnp.bfloat16),
            pltpu.VMEM((tiles, rows, slots * half), jnp.bfloat16),
            pltpu.VMEM(shape, jnp.bfloat16),
            pltpu.SemaphoreType.DMA((tiles,)),
            pltpu.SemaphoreType.DMA((tiles,)),
            pltpu.SemaphoreType.DMA((tiles,)),
        ],
        compiler_params=pltpu.CompilerParams(vmem_limit_bytes=60 << 20),
        cost_estimate=cost(2 * panel_rows * count * rows * slots * half, 6 << 20),
        name="first_product",
    )(near, named, x, values)


def merge_kernel(x_ref, o_ref, ids_ref, total, ids, sem):
    sources, height, half = x_ref.shape
    _, chunk, width = o_ref.shape
    slots = (height - 8) // chunk
    ids_ref[...] = x_ref[:, height - 8 :].astype(jnp.float32)[:, 0].astype(jnp.int32)
    copy = pltpu.make_async_copy(ids_ref, ids, sem)
    copy.start()
    total[...] = jnp.zeros_like(total)
    copy.wait()
    for source in range(sources):
        for slot in range(slots):
            piece = x_ref[source, slot * chunk : (slot + 1) * chunk]
            total[ids[source, slot]] += piece.astype(jnp.float32)
    blocks = width // half
    for panel in range(o_ref.shape[0]):
        for block in range(blocks):
            o_ref[panel, :, block * half : (block + 1) * half] = total[
                panel * blocks + block
            ].astype(jnp.bfloat16)


def merge(x, panels, blocks, chunk):
    sources, _, half = x.shape
    return pl.pallas_call(
        merge_kernel,
        in_specs=[VMEM],
        out_specs=[VMEM, VMEM],
        out_shape=[
            jax.ShapeDtypeStruct((panels, chunk, blocks * half), jnp.bfloat16),
            jax.ShapeDtypeStruct((sources, half), jnp.int32),
        ],
        scratch_shapes=[
            pltpu.VMEM((panels * blocks, chunk, half), jnp.float32),
            pltpu.SMEM((sources, half), jnp.int32),
            pltpu.SemaphoreType.DMA,
        ],
        compiler_params=pltpu.CompilerParams(vmem_limit_bytes=40 << 20),
        cost_estimate=cost(0, 8 << 20),
        name="merge",
    )(x)


def select_kernel(ids, x_ref, o_hbm, out, sem):
    sources, slots, chunk, half = out.shape
    blocks = x_ref.shape[2] // half
    groups = sem.shape[0]
    size = sources // groups

    def store(group):
        part = pl.ds(group * size, size)
        return pltpu.make_async_copy(out.at[part], o_hbm.at[part], sem.at[group])

    for group in range(groups):
        for source in range(group * size, (group + 1) * size):
            for slot in range(slots):
                block = ids[source * slots + slot]
                lanes = pl.ds(pl.multiple_of(lax.rem(block, blocks) * half, half), half)
                out[source, slot] = x_ref[lax.div(block, blocks), :, lanes]
        store(group).start()
    for group in range(groups):
        store(group).wait()


def select(ids, x, slots, half):
    sources, chunk, _ = x.shape
    shape = (sources, slots, chunk, half)
    return pl.pallas_call(
        select_kernel,
        in_specs=[SMEM, VMEM],
        out_specs=ANY,
        out_shape=pltpu.HBM(shape, jnp.bfloat16),
        scratch_shapes=[pltpu.VMEM(shape, jnp.bfloat16), pltpu.SemaphoreType.DMA((4,))],
        compiler_params=pltpu.CompilerParams(vmem_limit_bytes=40 << 20),
        cost_estimate=cost(0, 4 << 20),
        name="select",
    )(ids, x)


def near_kernel(near, place, x_ref, v_hbm, o_ref, other_ref, v, mine_ref, sem):
    parts, chunk, depth = x_ref.shape
    blocks, count, rows, half = v.shape

    def load(block):
        return pltpu.make_async_copy(v_hbm.at[block], v.at[block], sem.at[block])

    for block in range(blocks):
        load(block).start()
    mine_ref[...] = jnp.zeros_like(mine_ref)
    other_ref[...] = jnp.zeros_like(other_ref)
    mine = pl.multiple_of(place[0] * half, half)
    other = pl.multiple_of((1 - place[0]) * half, half)
    for block in range(blocks):
        load(block).wait()
        own = slice(block * half, (block + 1) * half)
        for q in range(count):
            target = pl.ds(pl.multiple_of(near[block, q] * half, half), half)
            mine_ref[own, target] = v[block, q, pl.ds(mine, half), :]
            other_ref[own, target] = v[block, q, pl.ds(other, half), :]
    side = parts // 2
    for part in range(2):
        o_ref[part * side * chunk : (part + 1) * side * chunk] = jnp.dot(
            x_ref[part * side : (part + 1) * side].reshape(side * chunk, depth),
            mine_ref[...],
            preferred_element_type=jnp.float32,
        )


def second_near(x, values, near, place):
    parts, chunk, depth = x.shape
    blocks, count, rows, half = values.shape
    columns = blocks * half
    return pl.pallas_call(
        near_kernel,
        in_specs=[SMEM, SMEM, VMEM, ANY],
        out_specs=[VMEM, VMEM],
        out_shape=[
            jax.ShapeDtypeStruct((parts * chunk, columns), jnp.float32),
            jax.ShapeDtypeStruct((depth, columns), jnp.bfloat16),
        ],
        scratch_shapes=[
            pltpu.VMEM(values.shape, jnp.bfloat16),
            pltpu.VMEM((depth, columns), jnp.bfloat16),
            pltpu.SemaphoreType.DMA((blocks,)),
        ],
        compiler_params=pltpu.CompilerParams(vmem_limit_bytes=40 << 20),
        cost_estimate=cost(2 * parts * chunk * depth * columns, 8 << 20),
        name="second_near",
    )(near, place, x, pltpu.with_memory_space_constraint(values, pltpu.HBM))


def far_kernel(x_ref, m_ref, near_ref, first_ref, second_ref, o_ref, sum_ref):
    parts, chunk, columns = o_ref.shape
    rows, half = parts * chunk, 128
    step = pl.program_id(0)
    left = x_ref[pl.ds(step * parts, parts)].reshape(rows, x_ref.shape[2])
    own = pl.ds(pl.multiple_of(step * rows, rows), rows)
    first = jnp.broadcast_to(first_ref[own, :], (rows, half))
    partial = None
    for pair in range(0, columns, 2 * half):
        far = jnp.dot(left, m_ref[:, pair : pair + 2 * half], preferred_element_type=jnp.float32)
        for at in (0, half):
            lanes = slice(pair + at, pair + at + half)
            value = jnp.exp(
                far[:, at : at + half] + near_ref[own, lanes] - first - second_ref[:, lanes]
            )
            partial = value if partial is None else partial + value
            rounded = jnp.minimum(value, LARGEST).astype(jnp.bfloat16)
            o_ref[:, :, lanes] = rounded.reshape(parts, chunk, half)
    sum_ref[0] = jnp.sum(partial.T, axis=0, keepdims=True)


def second_far(x, matrix, near, first, second, parts):
    col_count, chunk, depth = x.shape
    rows = parts * chunk
    columns = matrix.shape[1]
    steps = col_count // parts
    return pl.pallas_call(
        far_kernel,
        grid=(steps,),
        in_specs=[VMEM] * 5,
        out_specs=[
            pl.BlockSpec((parts, chunk, columns), lambda i: (i, 0, 0)),
            pl.BlockSpec((1, 1, rows), lambda i: (i, 0, 0)),
        ],
        out_shape=[
            pltpu.HBM((col_count, chunk, columns), jnp.bfloat16),
            jax.ShapeDtypeStruct((steps, 1, rows), jnp.float32),
        ],
        compiler_params=params(),
        cost_estimate=cost(2 * col_count * chunk * depth * columns, 10 << 20),
        name="second_far",
    )(x, matrix, near, first, second)


def colsum_kernel(s_ref, x_hbm, o_ref, x, sem):
    groups = sem.shape[0]
    parts, chunk, width = x.shape
    size = parts // groups

    def load(group):
        part = pl.ds(group * size, size)
        return pltpu.make_async_copy(x_hbm.at[part], x.at[part], sem.at[group])

    for group in range(groups):
        load(group).start()
    total = None
    for group in range(groups):
        load(group).wait()
        rows = slice(group * size * chunk, (group + 1) * size * chunk)
        term = jnp.dot(
            s_ref[:, rows],
            x[group * size : (group + 1) * size].reshape(size * chunk, width),
            preferred_element_type=jnp.float32,
        )
        total = term if total is None else total + term
    blocks, half = o_ref.shape
    line = total[0:1] + total[1:2] + total[2:3]
    for block in range(blocks):
        o_ref[block : block + 1] = line[:, block * half : (block + 1) * half]


def weighted_colsum(scale, x, blocks):
    parts, chunk, width = x.shape
    high = scale.astype(jnp.bfloat16)
    rest = scale - high.astype(jnp.float32)
    middle = rest.astype(jnp.bfloat16)
    low = (rest - middle.astype(jnp.float32)).astype(jnp.bfloat16)
    thirds = jnp.concatenate(
        [high[None], middle[None], low[None], jnp.zeros((13, scale.shape[0]), jnp.bfloat16)]
    )
    return pl.pallas_call(
        colsum_kernel,
        in_specs=[VMEM, ANY],
        out_specs=VMEM,
        out_shape=jax.ShapeDtypeStruct((blocks, width // blocks), jnp.float32),
        scratch_shapes=[pltpu.VMEM(x.shape, jnp.bfloat16), pltpu.SemaphoreType.DMA((4,))],
        compiler_params=pltpu.CompilerParams(vmem_limit_bytes=40 << 20),
        cost_estimate=cost(2 * 16 * parts * chunk * width, 4 << 20),
        name="weighted_colsum",
    )(thirds, pltpu.with_memory_space_constraint(x, pltpu.HBM))


def final_kernel(lines, x_ref, first_ref, second_ref, o_ref):
    step = pl.program_id(0)
    rows, slots, half = o_ref.shape
    chunk = x_ref.shape[2]
    for part in range(rows // chunk):
        at = step * (rows // chunk) + part
        first = first_ref[pl.ds(pl.multiple_of(at * chunk, chunk), chunk), :]
        first = jnp.broadcast_to(first, (chunk, half))
        values = [
            x_ref[at, slot].astype(jnp.float32) * first * second_ref[pl.ds(lines[slot], 1), :]
            for slot in range(slots)
        ]
        o_ref[part * chunk : (part + 1) * chunk] = jnp.swapaxes(jnp.stack(values), 0, 1).astype(
            jnp.bfloat16
        )


def final_scale(lines, x, first, second, parts):
    col_count, slots, chunk, half = x.shape
    steps = col_count // parts
    return pl.pallas_call(
        final_kernel,
        grid_spec=pltpu.PrefetchScalarGridSpec(
            num_scalar_prefetch=1,
            grid=(steps,),
            in_specs=[VMEM, VMEM, VMEM],
            out_specs=pl.BlockSpec((parts * chunk, slots, half), lambda i, n: (i, 0, 0)),
        ),
        out_shape=pltpu.HBM((col_count * chunk, slots, half), jnp.bfloat16),
        compiler_params=params(),
        cost_estimate=cost(0, 5 << 20),
        name="final_scale",
    )(lines, x, first, second)


def swap(value, axis, bit):
    size = lax.axis_size(axis)
    return lax.ppermute(value, axis, [(i, i ^ bit) for i in range(size)])


def move(value, by, bits):
    rows, cols, cores = (lax.axis_size(axis) for axis in ("row", "col", "pan"))
    pairs = [
        ((r * cols + c) * cores + h, ((r + by) % rows * cols + (c ^ bits[h])) * cores + h)
        for r in range(rows)
        for c in range(cols)
        for h in range(cores)
    ]
    return lax.ppermute(value, ("row", "col", "pan"), pairs)


def four(value, low, by):
    return [value] + [move(value, by, (k * low, k * low)) for k in (1, 2, 3)]


def shared_pairs(value, low, by):
    return move(value, by, (0, low)), move(value, by, (2 * low, 3 * low))


def shared_sum(value, low, by):
    first, second = shared_pairs(value, low, by)
    both = first + second
    return both + swap(both, "pan", 1)


def local(
    plan_values,
    plan_blocks,
    first_values,
    first_blocks,
    second_values,
    second_blocks,
    weight_first,
    weight_second,
    offset_first,
    offset_second,
):
    col_count = lax.axis_size("col")
    column = lax.axis_index("col")
    side = lax.axis_index("pan")
    blocks_here = second_blocks.shape[0]
    panel_rows, slots, half = plan_values.shape
    block_size = first_values.shape[2]
    chunk = panel_rows // col_count
    plan_width = float(slots * col_count * block_size)

    named = plan_blocks[0]
    product = first_product(plan_values, first_values, first_blocks, named, col_count)
    arrived = lax.all_to_all(product, "col", split_axis=0, concat_axis=0, tiled=True)
    merged, ids = merge(arrived, col_count, blocks_here, chunk)
    merged, offset_first, offset_second = lax.optimization_barrier(
        (merged, offset_first, offset_second)
    )
    mine = lax.all_to_all(merged, "col", split_axis=0, concat_axis=0, tiled=True)
    ids = ids[:, :slots].reshape(-1)
    own_blocks = column * blocks_here + jnp.arange(blocks_here)
    present = jnp.any(ids[:, None] == own_blocks[None, :], axis=0)
    other = swap(mine, "pan", 1)
    near, matrix_other = second_near(mine, second_values, second_blocks, side.reshape(1))
    offsets = jnp.where(present[:, None], offset_second, jnp.inf).reshape(1, -1)
    kernel, totals = second_far(other, matrix_other, near, offset_first[:, None], offsets, 8)
    back = lax.all_to_all(kernel, "col", split_axis=0, concat_axis=0, tiled=True)

    totals = totals.reshape(blocks_here, -1)
    totals = totals + swap(totals, "pan", 1)
    totals = shared_sum(totals, 1, 1)
    totals = shared_sum(totals, 4, -1)
    scale_first = weight_first * plan_width / totals.reshape(-1)
    colsum = weighted_colsum(scale_first, kernel, blocks_here)
    sums = jnp.concatenate(
        [colsum, jnp.broadcast_to(present.astype(jnp.float32)[:, None], colsum.shape)]
    )
    sums = sums + swap(sums, "row", 1)
    sums = sums + swap(sums, "row", 2)
    ids, sums = lax.optimization_barrier((ids, sums))
    sums = sums + swap(sums, "row", 7)
    colsum = sums[:blocks_here]
    counts = sums[blocks_here:, :1] * float(panel_rows)
    scale_second = weight_second * counts / jnp.where(counts > 0, colsum, 1.0)
    all_second = jnp.concatenate(four(scale_second, 1, 1))
    all_second = jnp.concatenate(four(all_second, 4, 1))
    lines = ((named // blocks_here) ^ column) * blocks_here + named % blocks_here

    chosen = select(ids, back, slots, half)
    home = lax.all_to_all(chosen, "col", split_axis=0, concat_axis=0, tiled=True)
    new_plan = final_scale(lines, home, scale_first[:, None], all_second, 4)
    return (new_plan, scale_first, scale_second)


def solution(mesh):
    return jax.shard_map(
        local,
        mesh=mesh,
        in_specs=(
            P("row", "col", "pan"),
            P("row", "col"),
            P("row", None, None, None),
            P("row", None),
            P("col", None, None, "pan"),
            P("col", None),
            P("row"),
            P("col", "pan"),
            P("row"),
            P("col", "pan"),
        ),
        out_specs=(P("row", "col", "pan"), P("row"), P("col", "pan")),
        check_vma=False,
    )
```

time: 443 us -> 168 us (0.38)
  waiting for transfers between devices: 137 us -> 22 us
  blocking collectives: 178 us -> 66.8 us
  matrix products: 47.4 us -> 0 us
  local copies, waits for them, and re-layouts: 40.8 us -> 0.76 us
  starting transfers between devices: 14.5 us -> 50.6 us
  Pallas kernels: 0 us -> 25.6 us
  between operations: 14.3 us -> 0.89 us
  other arithmetic: 10 us -> 0.84 us
    all_to_all x2, waiting for transfers between devices: 121 us -> 1.92 us  [the longest x1 1.92 us: local(): lax.all_to_all(kernel, 'col', split_axis=0, concat_axis=0, tiled=True)]
    psum x2 -> x0, blocking collectives: 83.9 us -> none  [the longest x1 67.6 us: local(): row_totals = lax.psum(jnp.sum(kernel_values, axis=(1, 2)), ('col', 'pan'))]
    dot_general x9 -> x0, matrix products: 47.4 us -> none  [the longest x1 10.1 us: second_product(): jnp.einsum('rkb,kblh->rlh', dense_plan, panel_matrix, preferred_element_t...]
    ppermute x0 -> x17, starting transfers between devices: none -> 42 us  [the longest x10 30.7 us: move(): return lax.ppermute(value, ('row', 'col', 'pan'), pairs)]
    all_to_all x1 -> x2, blocking collectives: 93.6 us -> 66.8 us  [the longest x1 35.9 us: local(): lax.all_to_all(product, 'col', split_axis=0, concat_axis=0, tiled=True)]
    pallas_call x0 -> x7, Pallas kernels: none -> 25.6 us  [the longest x1 5.92 us: first_product(): pl.pallas_call(first_kernel, in_specs=[SMEM, SMEM, ANY, ANY], out_specs=A...]
    ppermute x0 -> x17, waiting for transfers between devices: none -> 20 us  [the longest x10 11.9 us: move(): return lax.ppermute(value, ('row', 'col', 'pan'), pairs)]
    all_gather x1 -> x0, waiting for transfers between devices: 15.7 us -> none  [local(): gathered = lax.all_gather(dense_plan, 'pan', axis=2, tiled=True)]
  transfers between devices with their start and end apart: 3 -> 19, of which waited for: 2 -> 12; matrix products, arithmetic and copies ran while one was open for 11% -> 1% of each run, Pallas kernels for 0% -> 4%
where the time goes in v2:
time: 168 us; the launch traced here: 167 us
  blocking collectives  66.8 us (40%)
  starting transfers between devices  50.6 us (30%)
  Pallas kernels  25.6 us (15%)
  waiting for transfers between devices  22 us (13%)
    all_to_all x1, blocking collectives, local(): lax.all_to_all(product, 'col', split_axis=0, concat_axis=0, tiled=True)  35.9 us
    all_to_all x1, blocking collectives, local(): lax.all_to_all(merged, 'col', split_axis=0, concat_axis=0, tiled=True)  30.9 us
    ppermute x10, starting transfers between devices, move(): return lax.ppermute(value, ('row', 'col', 'pan'), pairs)  30.7 us
    ppermute x10, waiting for transfers between devices, move(): return lax.ppermute(value, ('row', 'col', 'pan'), pairs)  11.9 us
    ppermute x7, starting transfers between devices, swap(): return lax.ppermute(value, axis, [(i, i ^ bit) for i in range(size)])  11.3 us
    ppermute x7, waiting for transfers between devices, swap(): return lax.ppermute(value, axis, [(i, i ^ bit) for i in range(size)])  8.14 us
    pallas_call x1, Pallas kernels, first_product(): pl.pallas_call(first_kernel, in_specs=[SMEM, SMEM, ANY, ANY], out_specs=A...  5.92 us
    pallas_call x1, Pallas kernels, second_far(): pl.pallas_call(far_kernel, grid=(steps,), in_specs=[VMEM] * 5, out_specs=...  5.83 us
  transfers between devices with their start and end apart: 19, of which 12 were waited for; matrix products, arithmetic and copies ran while one was open for 1% of the time, Pallas kernels for 4%

profile of v2, /device:TPU:32, one launch (start us, length us, event | category | flops | bytes accessed | tf_op | source)
XLA Modules:
  0.0 167.5 jit_solution(5937984237923610220)
XLA Ops:
  0.6 5.9 %first_product.1 = bf16[16,520,128]{2,1,0:T(8,128)(2,1)} custom-call(s32[4,3]{1,0:T(4,128)} %near.2, s32[8]{0:T(128)} %bitcast.17, bf16[1024,8,128]{2,1,0:T(8,128)(2,1)} %x_hbm.1, bf16[4,3,256,256]{3,2,1,0:T(8,128)(2,1)} %c_hbm.1), custom_call_target="tpu_custom_call" | custom-call | flops 1610612736 | bytes 6291456 | tf_op jit(solution)/shard_map/first_product/pallas_call | solution.py:79
  6.6 35.9 %all_to_all.20.x_ref = bf16[16,520,128]{2,1,0:T(8,128)(2,1)S(1)} all-to-all(bf16[16,520,128]{2,1,0:T(8,128)(2,1)} %first_product.1), channel_id=1, replica_groups=mesh['row'=8,'col'=16,'pan'=2] {'col'}, dimensions={0} | all-to-all | bytes 4259840 | tf_op jit(solution)/shard_map/all_to_all | solution.py:409
  42.5 1.9 %merge.1 = (bf16[16,64,1024]{2,1,0:T(8,128)(2,1)S(1)}, s32[16,128]{1,0:T(8,128)S(1)}) custom-call(bf16[16,520,128]{2,1,0:T(8,128)(2,1)S(1)} %all_to_all.20.x_ref), custom_call_target="tpu_custom_call" | custom-call | bytes 8388608 | tf_op jit(solution)/shard_map/merge/pallas_call | solution.py:122
  44.4 30.9 %all_to_all.21.x_ref = bf16[16,64,1024]{2,1,0:T(8,128)(2,1)S(1)} all-to-all(bf16[16,64,1024]{2,1,0:T(8,128)(2,1)S(1)} %get-tuple-element.16), channel_id=1, replica_groups=mesh['row'=8,'col'=16,'pan'=2] {'col'}, dimensions={0} | all-to-all | bytes 4194304 | tf_op jit(solution)/shard_map/all_to_all | solution.py:414
  75.3 0.1 reshape.30.ids
  75.4 0.2 copy.15.first_ref
  75.7 0.2 compare_reduce_fusion.1
  75.9 0.1 broadcast_select_fusion
  75.9 4.9 %second_near.1 = (f32[1024,1024]{1,0:T(8,128)S(1)}, bf16[1024,1024]{1,0:T(8,128)(2,1)S(1)}) custom-call(s32[8,6]{1,0:T(8,128)S(1)} %copy-done, s32[1]{0:T(128)} %bitcast.1.place, bf16[16,64,1024]{2,1,0:T(8,128)(2,1)S(1)} %all_to_all.21.x_ref, bf16[8,6,256,128]{3,2,1,0:T(8,128)(2,1)} %v_hbm.1), custom_call_target="tpu_custom_call" | custom-call | flops 2147483648 | bytes 8388608 | tf_op jit(solution)/shard_map/second_near/pallas_call | solution.py:210
  80.9 5.8 %second_far.1 = (bf16[16,64,1024]{2,1,0:T(8,128)(2,1)}, f32[2,1,512]{2,1,0:T(1,128)S(1)}) custom-call(bf16[16,64,1024]{2,1,0:T(8,128)(2,1)} %collective-permute-done.x_ref, bf16[1024,1024]{1,0:T(8,128)(2,1)S(1)} %get-tuple-element.17.m_ref, f32[1024,1024]{1,0:T(8,128)S(1)} %get-tuple-element.18.near_ref, f32[1024,1]{1,0:T(8,128)S(1)} %copy.15.first_ref, ...), custom_call_target="tpu_custom_call" | custom-call | flops 2147483648 | bytes 10485760 | tf_op jit(solution)/shard_map/second_far/pallas_call | solution.py:255
  86.7 3.9 %all-to-all-start.2 = ((bf16[16,64,1024]{2,1,0:T(8,128)(2,1)}), bf16[16,64,1024]{2,1,0:T(8,128)(2,1)S(1)}, u32[]{:S(2)}, u32[]{:S(2)}) async-start(bf16[16,64,1024]{2,1,0:T(8,128)(2,1)} %get-tuple-element.22.x_hbm), calls=%async_computation.2 | async-start | bytes 4194304 | tf_op jit(solution)/shard_map/all_to_all | solution.py:422
  90.6 0.6 collective-permute-start.1
  91.2 0.8 collective-permute-done.1
  92.0 1.9 %collective-permute-start.2 = (f32[8,128]{1,0:T(8,128)S(1)}, f32[8,128]{1,0:T(8,128)S(1)}, u32[]{:S(2)}, u32[]{:S(2)}) collective-permute-start(f32[8,128]{1,0:T(8,128)S(1)} %add.48), channel_id=1, source_target_pairs={{0,32},{1,35},{2,34},{3,33},{4,36},{5,39},{6,38},{7,37},{8,40},{9,... | collective-permute-start | bytes 12296 | tf_op jit(solution)/shard_map/ppermute | solution.py:369
  93.9 4.4 %collective-permute-start.3 = (f32[8,128]{1,0:T(8,128)S(1)}, f32[8,128]{1,0:T(8,128)S(1)}, u32[]{:S(2)}, u32[]{:S(2)}) collective-permute-start(f32[8,128]{1,0:T(8,128)S(1)} %add.48), channel_id=1, source_target_pairs={{0,36},{1,39},{2,38},{3,37},{4,32},{5,35},{6,34},{7,33},{8,44},{9,... | collective-permute-start | bytes 12296 | tf_op jit(solution)/shard_map/ppermute | solution.py:369
  98.3 1.8 %collective-permute-done.3 = f32[8,128]{1,0:T(8,128)S(1)} collective-permute-done((f32[8,128]{1,0:T(8,128)S(1)}, f32[8,128]{1,0:T(8,128)S(1)}, u32[]{:S(2)}, u32[]{:S(2)}) %collective-permute-start.3) | collective-permute-done | bytes 4128 | tf_op jit(solution)/shard_map/ppermute | solution.py:369
  100.1 1.2 collective-permute-done.4
  101.3 2.1 %collective-permute-start.5 = (f32[8,128]{1,0:T(8,128)S(1)}, f32[8,128]{1,0:T(8,128)S(1)}, u32[]{:S(2)}, u32[]{:S(2)}) collective-permute-start(f32[8,128]{1,0:T(8,128)S(1)} %add.50), channel_id=1, source_target_pairs={{0,224},{1,233},{2,226},{3,235},{4,228},{5,237},{6,230},{7,239},{8... | collective-permute-start | bytes 12296 | tf_op jit(solution)/shard_map/ppermute | solution.py:369
  103.4 4.5 %collective-permute-start.6 = (f32[8,128]{1,0:T(8,128)S(1)}, f32[8,128]{1,0:T(8,128)S(1)}, u32[]{:S(2)}, u32[]{:S(2)}) collective-permute-start(f32[8,128]{1,0:T(8,128)S(1)} %add.50), channel_id=1, source_target_pairs={{0,240},{1,249},{2,242},{3,251},{4,244},{5,253},{6,246},{7,255},{8... | collective-permute-start | bytes 12296 | tf_op jit(solution)/shard_map/ppermute | solution.py:369
  107.9 3.1 %collective-permute-done.6 = f32[8,128]{1,0:T(8,128)S(1)} collective-permute-done((f32[8,128]{1,0:T(8,128)S(1)}, f32[8,128]{1,0:T(8,128)S(1)}, u32[]{:S(2)}, u32[]{:S(2)}) %collective-permute-start.6) | collective-permute-done | bytes 4128 | tf_op jit(solution)/shard_map/ppermute | solution.py:369
  111.0 0.1 pad.9.clone
  111.1 0.1 pad.5.clone
  111.2 1.0 collective-permute-done.7
  112.3 0.1 maximum_maximum_fusion.s_ref
  112.3 1.7 %weighted_colsum.1 = f32[8,128]{1,0:T(8,128)S(1)} custom-call(bf16[16,1024]{1,0:T(8,128)(2,1)S(1)} %maximum_maximum_fusion.s_ref, bf16[16,64,1024]{2,1,0:T(8,128)(2,1)} %get-tuple-element.22.x_hbm), custom_call_target="tpu_custom_call" | custom-call | flops 33554432 | bytes 4194304 | tf_op jit(solution)/shard_map/weighted_colsum/pallas_call | solution.py:309
  114.2 1.9 %collective-permute-start.8 = (f32[16,128]{1,0:T(8,128)S(1)}, f32[16,128]{1,0:T(8,128)S(1)}, u32[]{:S(2)}, u32[]{:S(2)}) collective-permute-start(f32[16,128]{1,0:T(8,128)S(1)} %pad_maximum_fusion.1), channel_id=1, source_target_pairs={{0,32},{32,0},{64,96},{96,64},{128,160},{160,128},{192,224},{224,1... | collective-permute-start | bytes 24584 | tf_op jit(solution)/shard_map/ppermute | solution.py:358
  116.1 1.7 %collective-permute-done.8 = f32[16,128]{1,0:T(8,128)S(1)} collective-permute-done((f32[16,128]{1,0:T(8,128)S(1)}, f32[16,128]{1,0:T(8,128)S(1)}, u32[]{:S(2)}, u32[]{:S(2)}) %collective-permute-start.8) | collective-permute-done | bytes 8224 | tf_op jit(solution)/shard_map/ppermute | solution.py:358
  117.9 3.8 %collective-permute-start.9 = (f32[16,128]{1,0:T(8,128)S(1)}, f32[16,128]{1,0:T(8,128)S(1)}, u32[]{:S(2)}, u32[]{:S(2)}) collective-permute-start(f32[16,128]{1,0:T(8,128)S(1)} %fusion.4), channel_id=1, source_target_pairs={{0,64},{32,96},{64,0},{96,32},{128,192},{160,224},{192,128},{224,1... | collective-permute-start | bytes 24584 | tf_op jit(solution)/shard_map/ppermute | solution.py:358
  121.7 1.6 collective-permute-done.9
  123.3 1.9 %all-to-all-done.2.x_ref = bf16[16,64,1024]{2,1,0:T(8,128)(2,1)S(1)} async-done(((bf16[16,64,1024]{2,1,0:T(8,128)(2,1)}), bf16[16,64,1024]{2,1,0:T(8,128)(2,1)S(1)}, u32[]{:S(2)}, u32[]{:S(2)}) %all-to-all-start.2) | async-done | bytes 2097184 | tf_op jit(solution)/shard_map/all_to_all | solution.py:422
  125.2 2.0 %select.7 = bf16[16,8,64,128]{3,2,1,0:T(8,128)(2,1)} custom-call(s32[128]{0:T(128)S(1)} %reshape.30.ids, bf16[16,64,1024]{2,1,0:T(8,128)(2,1)S(1)} %all-to-all-done.2.x_ref), custom_call_target="tpu_custom_call" | custom-call | bytes 4194304 | tf_op jit(solution)/shard_map/select/pallas_call | solution.py:165
  127.3 4.8 %all-to-all-start.3 = ((bf16[16,8,64,128]{3,2,1,0:T(8,128)(2,1)}), bf16[16,8,64,128]{3,2,1,0:T(8,128)(2,1)S(1)}, u32[]{:S(2)}, u32[]{:S(2)}) async-start(bf16[16,8,64,128]{3,2,1,0:T(8,128)(2,1)} %select.7), calls=%async_computation.3 | async-start | bytes 4194304 | tf_op jit(solution)/shard_map/all_to_all | solution.py:445
  132.1 5.0 %collective-permute-start.10 = (f32[16,128]{1,0:T(8,128)S(1)}, f32[16,128]{1,0:T(8,128)S(1)}, u32[]{:S(2)}, u32[]{:S(2)}) collective-permute-start(f32[16,128]{1,0:T(8,128)S(1)} %add.54), channel_id=1, source_target_pairs={{0,224},{32,192},{64,160},{96,128},{128,96},{160,64},{192,32},{224... | collective-permute-start | bytes 24584 | tf_op jit(solution)/shard_map/ppermute | solution.py:358
  137.0 1.8 %collective-permute-done.10 = f32[16,128]{1,0:T(8,128)S(1)} collective-permute-done((f32[16,128]{1,0:T(8,128)S(1)}, f32[16,128]{1,0:T(8,128)S(1)}, u32[]{:S(2)}, u32[]{:S(2)}) %collective-permute-start.10) | collective-permute-done | bytes 8224 | tf_op jit(solution)/shard_map/ppermute | solution.py:358
  138.8 0.1 fusion.1
  138.9 0.1 compare_reduce_fusion
  139.0 0.1 constant_dynamic-update-slice_fusion.6
  139.1 2.8 %collective-permute-start.11 = (f32[8,128]{1,0:T(8,128)S(1)}, f32[8,128]{1,0:T(8,128)S(1)}, u32[]{:S(2)}, u32[]{:S(2)}) collective-permute-start(f32[8,128]{1,0:T(8,128)S(1)} %get-tuple-element.26), channel_id=1, source_target_pairs={{0,34},{1,35},{2,32},{3,33},{4,38},{5,39},{6,36},{7,37},{8,42},{9,... | collective-permute-start | bytes 12296 | tf_op jit(solution)/shard_map/ppermute | solution.py:369
  141.9 2.3 %collective-permute-start.12 = (f32[8,128]{1,0:T(8,128)S(1)}, f32[8,128]{1,0:T(8,128)S(1)}, u32[]{:S(2)}, u32[]{:S(2)}) collective-permute-start(f32[8,128]{1,0:T(8,128)S(1)} %get-tuple-element.26), channel_id=1, source_target_pairs={{0,36},{1,37},{2,38},{3,39},{4,32},{5,33},{6,34},{7,35},{8,44},{9,... | collective-permute-start | bytes 12296 | tf_op jit(solution)/shard_map/ppermute | solution.py:369
  144.2 2.2 %collective-permute-start.13 = (f32[8,128]{1,0:T(8,128)S(1)}, f32[8,128]{1,0:T(8,128)S(1)}, u32[]{:S(2)}, u32[]{:S(2)}) collective-permute-start(f32[8,128]{1,0:T(8,128)S(1)} %get-tuple-element.26), channel_id=1, source_target_pairs={{0,38},{1,39},{2,36},{3,37},{4,34},{5,35},{6,32},{7,33},{8,46},{9,... | collective-permute-start | bytes 12296 | tf_op jit(solution)/shard_map/ppermute | solution.py:369
  146.4 0.2 copy.16.first_ref
  146.7 1.4 collective-permute-done.12
  148.0 2.0 %collective-permute-done.13 = f32[8,128]{1,0:T(8,128)S(1)} collective-permute-done((f32[8,128]{1,0:T(8,128)S(1)}, f32[8,128]{1,0:T(8,128)S(1)}, u32[]{:S(2)}, u32[]{:S(2)}) %collective-permute-start.13) | collective-permute-done | bytes 4128 | tf_op jit(solution)/shard_map/ppermute | solution.py:369
  150.0 3.4 %collective-permute-start.14 = (f32[32,128]{1,0:T(8,128)S(1)}, f32[32,128]{1,0:T(8,128)S(1)}, u32[]{:S(2)}, u32[]{:S(2)}) collective-permute-start(f32[32,128]{1,0:T(8,128)S(1)} %pad_maximum_fusion), channel_id=1, source_target_pairs={{0,40},{1,41},{2,42},{3,43},{4,44},{5,45},{6,46},{7,47},{8,32},{9,... | collective-permute-start | bytes 49160 | tf_op jit(solution)/shard_map/ppermute | solution.py:369
  153.4 5.0 %collective-permute-start.15 = (f32[32,128]{1,0:T(8,128)S(1)}, f32[32,128]{1,0:T(8,128)S(1)}, u32[]{:S(2)}, u32[]{:S(2)}) collective-permute-start(f32[32,128]{1,0:T(8,128)S(1)} %pad_maximum_fusion), channel_id=1, source_target_pairs={{0,48},{1,49},{2,50},{3,51},{4,52},{5,53},{6,54},{7,55},{8,56},{9,... | collective-permute-start | bytes 49160 | tf_op jit(solution)/shard_map/ppermute | solution.py:369
  158.4 2.2 %collective-permute-start.16 = (f32[32,128]{1,0:T(8,128)S(1)}, f32[32,128]{1,0:T(8,128)S(1)}, u32[]{:S(2)}, u32[]{:S(2)}) collective-permute-start(f32[32,128]{1,0:T(8,128)S(1)} %pad_maximum_fusion), channel_id=1, source_target_pairs={{0,56},{1,57},{2,58},{3,59},{4,60},{5,61},{6,62},{7,63},{8,48},{9,... | collective-permute-start | bytes 49160 | tf_op jit(solution)/shard_map/ppermute | solution.py:369
  160.7 3.6 %collective-permute-done.16 = f32[32,128]{1,0:T(8,128)S(1)} collective-permute-done((f32[32,128]{1,0:T(8,128)S(1)}, f32[32,128]{1,0:T(8,128)S(1)}, u32[]{:S(2)}, u32[]{:S(2)}) %collective-permute-start.16) | collective-permute-done | bytes 16416 | tf_op jit(solution)/shard_map/ppermute | solution.py:369
  164.2 3.3 %final_scale.1 = bf16[1024,8,128]{2,1,0:T(8,128)(2,1)} custom-call(s32[8]{0:T(128)S(1)} %fusion.3.lines, bf16[16,8,64,128]{3,2,1,0:T(8,128)(2,1)S(1)} %all-to-all-done.3.x_ref, f32[1024,1]{1,0:T(8,128)S(1)} %copy.16.first_ref, f32[128,128]{1,0:T(8,128)S(1)} %constant_dynamic-update-slice_fusion.second_ref), custom_call_target="tpu_custom_call" | custom-call | bytes 5242880 | tf_op jit(solution)/shard_map/final_scale/pallas_call | solution.py:341
  (50 shorter events, 0.3 us)
Async XLA Ops:
  44.4 31.0 %copy-start.3 = (f32[1024]{0:T(1024)S(1)}, f32[1024]{0:T(1024)}, u32[]{:S(2)}) copy-start(f32[1024]{0:T(1024)} %param.18) | copy-start | bytes 12292
  44.4 31.4 %copy-start.5 = (f32[8,128]{1,0:T(8,128)S(1)}, f32[8,128]{1,0:T(8,128)}, u32[]{:S(2)}) copy-start(f32[8,128]{1,0:T(8,128)} %param.19) | copy-start | bytes 12292
  44.4 31.5 %copy-start = (s32[8,6]{1,0:T(8,128)S(1)}, s32[8,6]{1,0:T(8,128)}, u32[]{:S(2)}) copy-start(s32[8,6]{1,0:T(8,128)} %near.3) | copy-start | bytes 580
  75.3 5.6 %collective-permute-start = (bf16[16,64,1024]{2,1,0:T(8,128)(2,1)S(1)}, bf16[16,64,1024]{2,1,0:T(8,128)(2,1)}, u32[]{:S(2)}, u32[]{:S(2)}) collective-permute-start(bf16[16,64,1024]{2,1,0:T(8,128)(2,1)S(1)} %all_to_all.21.x_ref), channel_id=1, source_target_pairs={{0,1},{1,0},{2,3},{3,2},{4,5},{5,4},{6,7},{7,6},{8,9},{9,8},{10,11... | collective-permute-start | bytes 6291464 | tf_op jit(solution)/shard_map/ppermute | solution.py:358
  86.7 25.5 %copy-start.6 = (f32[1024]{0:T(1024)S(1)}, f32[1024]{0:T(1024)}, u32[]{:S(2)}) copy-start(f32[1024]{0:T(1024)} %param.16) | copy-start | bytes 12292
  86.7 38.5 %all-to-all-start.2 = ((bf16[16,64,1024]{2,1,0:T(8,128)(2,1)}), bf16[16,64,1024]{2,1,0:T(8,128)(2,1)S(1)}, u32[]{:S(2)}, u32[]{:S(2)}) async-start(bf16[16,64,1024]{2,1,0:T(8,128)(2,1)} %get-tuple-element.22.x_hbm), calls=%async_computation.2 | async-start | bytes 4194304 | tf_op jit(solution)/shard_map/all_to_all | solution.py:422
  90.6 1.4 collective-permute-start.1
  92.0 6.3 %collective-permute-start.2 = (f32[8,128]{1,0:T(8,128)S(1)}, f32[8,128]{1,0:T(8,128)S(1)}, u32[]{:S(2)}, u32[]{:S(2)}) collective-permute-start(f32[8,128]{1,0:T(8,128)S(1)} %add.48), channel_id=1, source_target_pairs={{0,32},{1,35},{2,34},{3,33},{4,36},{5,39},{6,38},{7,37},{8,40},{9,... | collective-permute-start | bytes 12296 | tf_op jit(solution)/shard_map/ppermute | solution.py:369
  93.9 6.2 %collective-permute-start.3 = (f32[8,128]{1,0:T(8,128)S(1)}, f32[8,128]{1,0:T(8,128)S(1)}, u32[]{:S(2)}, u32[]{:S(2)}) collective-permute-start(f32[8,128]{1,0:T(8,128)S(1)} %add.48), channel_id=1, source_target_pairs={{0,36},{1,39},{2,38},{3,37},{4,32},{5,35},{6,34},{7,33},{8,44},{9,... | collective-permute-start | bytes 12296 | tf_op jit(solution)/shard_map/ppermute | solution.py:369
  100.1 1.2 collective-permute-start.4
  101.3 6.6 %collective-permute-start.5 = (f32[8,128]{1,0:T(8,128)S(1)}, f32[8,128]{1,0:T(8,128)S(1)}, u32[]{:S(2)}, u32[]{:S(2)}) collective-permute-start(f32[8,128]{1,0:T(8,128)S(1)} %add.50), channel_id=1, source_target_pairs={{0,224},{1,233},{2,226},{3,235},{4,228},{5,237},{6,230},{7,239},{8... | collective-permute-start | bytes 12296 | tf_op jit(solution)/shard_map/ppermute | solution.py:369
  103.4 7.6 %collective-permute-start.6 = (f32[8,128]{1,0:T(8,128)S(1)}, f32[8,128]{1,0:T(8,128)S(1)}, u32[]{:S(2)}, u32[]{:S(2)}) collective-permute-start(f32[8,128]{1,0:T(8,128)S(1)} %add.50), channel_id=1, source_target_pairs={{0,240},{1,249},{2,242},{3,251},{4,244},{5,253},{6,246},{7,255},{8... | collective-permute-start | bytes 12296 | tf_op jit(solution)/shard_map/ppermute | solution.py:369
  111.0 1.2 collective-permute-start.7
  112.2 34.2 %copy-start.1 = (f32[1024]{0:T(1024)}, f32[1024]{0:T(1024)S(1)}, u32[]{:S(2)}) copy-start(f32[1024]{0:T(1024)S(1)} %get-tuple-element.28) | copy-start | bytes 12292
  114.2 3.7 %collective-permute-start.8 = (f32[16,128]{1,0:T(8,128)S(1)}, f32[16,128]{1,0:T(8,128)S(1)}, u32[]{:S(2)}, u32[]{:S(2)}) collective-permute-start(f32[16,128]{1,0:T(8,128)S(1)} %pad_maximum_fusion.1), channel_id=1, source_target_pairs={{0,32},{32,0},{64,96},{96,64},{128,160},{160,128},{192,224},{224,1... | collective-permute-start | bytes 24584 | tf_op jit(solution)/shard_map/ppermute | solution.py:358
  117.9 5.4 %collective-permute-start.9 = (f32[16,128]{1,0:T(8,128)S(1)}, f32[16,128]{1,0:T(8,128)S(1)}, u32[]{:S(2)}, u32[]{:S(2)}) collective-permute-start(f32[16,128]{1,0:T(8,128)S(1)} %fusion.4), channel_id=1, source_target_pairs={{0,64},{32,96},{64,0},{96,32},{128,192},{160,224},{192,128},{224,1... | collective-permute-start | bytes 24584 | tf_op jit(solution)/shard_map/ppermute | solution.py:358
  127.3 11.8 %copy-start.4 = (f32[8,128]{1,0:T(8,128)S(1)}, f32[8,128]{1,0:T(8,128)}, u32[]{:S(2)}) copy-start(f32[8,128]{1,0:T(8,128)} %param.17) | copy-start | bytes 12292
  127.3 19.1 %copy-start.7 = (s32[1,8]{1,0:T(1,128)S(1)}, s32[1,8]{1,0:T(1,128)}, u32[]{:S(2)}) copy-start(s32[1,8]{1,0:T(1,128)} %param.11) | copy-start | bytes 100
  127.3 36.9 %all-to-all-start.3 = ((bf16[16,8,64,128]{3,2,1,0:T(8,128)(2,1)}), bf16[16,8,64,128]{3,2,1,0:T(8,128)(2,1)S(1)}, u32[]{:S(2)}, u32[]{:S(2)}) async-start(bf16[16,8,64,128]{3,2,1,0:T(8,128)(2,1)} %select.7), calls=%async_computation.3 | async-start | bytes 4194304 | tf_op jit(solution)/shard_map/all_to_all | solution.py:445
  132.1 6.7 %collective-permute-start.10 = (f32[16,128]{1,0:T(8,128)S(1)}, f32[16,128]{1,0:T(8,128)S(1)}, u32[]{:S(2)}, u32[]{:S(2)}) collective-permute-start(f32[16,128]{1,0:T(8,128)S(1)} %add.54), channel_id=1, source_target_pairs={{0,224},{32,192},{64,160},{96,128},{128,96},{160,64},{192,32},{224... | collective-permute-start | bytes 24584 | tf_op jit(solution)/shard_map/ppermute | solution.py:358
  139.1 28.4 %copy-start.2 = (f32[8,128]{1,0:T(8,128)}, f32[8,128]{1,0:T(8,128)S(1)}, u32[]{:S(2)}) copy-start(f32[8,128]{1,0:T(8,128)S(1)} %get-tuple-element.26) | copy-start | bytes 12292
  139.1 7.5 %collective-permute-start.11 = (f32[8,128]{1,0:T(8,128)S(1)}, f32[8,128]{1,0:T(8,128)S(1)}, u32[]{:S(2)}, u32[]{:S(2)}) collective-permute-start(f32[8,128]{1,0:T(8,128)S(1)} %get-tuple-element.26), channel_id=1, source_target_pairs={{0,34},{1,35},{2,32},{3,33},{4,38},{5,39},{6,36},{7,37},{8,42},{9,... | collective-permute-start | bytes 12296 | tf_op jit(solution)/shard_map/ppermute | solution.py:369
  141.9 6.1 %collective-permute-start.12 = (f32[8,128]{1,0:T(8,128)S(1)}, f32[8,128]{1,0:T(8,128)S(1)}, u32[]{:S(2)}, u32[]{:S(2)}) collective-permute-start(f32[8,128]{1,0:T(8,128)S(1)} %get-tuple-element.26), channel_id=1, source_target_pairs={{0,36},{1,37},{2,38},{3,39},{4,32},{5,33},{6,34},{7,35},{8,44},{9,... | collective-permute-start | bytes 12296 | tf_op jit(solution)/shard_map/ppermute | solution.py:369
  144.2 5.8 %collective-permute-start.13 = (f32[8,128]{1,0:T(8,128)S(1)}, f32[8,128]{1,0:T(8,128)S(1)}, u32[]{:S(2)}, u32[]{:S(2)}) collective-permute-start(f32[8,128]{1,0:T(8,128)S(1)} %get-tuple-element.26), channel_id=1, source_target_pairs={{0,38},{1,39},{2,36},{3,37},{4,34},{5,35},{6,32},{7,33},{8,46},{9,... | collective-permute-start | bytes 12296 | tf_op jit(solution)/shard_map/ppermute | solution.py:369
  150.0 10.6 %collective-permute-start.14 = (f32[32,128]{1,0:T(8,128)S(1)}, f32[32,128]{1,0:T(8,128)S(1)}, u32[]{:S(2)}, u32[]{:S(2)}) collective-permute-start(f32[32,128]{1,0:T(8,128)S(1)} %pad_maximum_fusion), channel_id=1, source_target_pairs={{0,40},{1,41},{2,42},{3,43},{4,44},{5,45},{6,46},{7,47},{8,32},{9,... | collective-permute-start | bytes 49160 | tf_op jit(solution)/shard_map/ppermute | solution.py:369
  153.4 7.2 %collective-permute-start.15 = (f32[32,128]{1,0:T(8,128)S(1)}, f32[32,128]{1,0:T(8,128)S(1)}, u32[]{:S(2)}, u32[]{:S(2)}) collective-permute-start(f32[32,128]{1,0:T(8,128)S(1)} %pad_maximum_fusion), channel_id=1, source_target_pairs={{0,48},{1,49},{2,50},{3,51},{4,52},{5,53},{6,54},{7,55},{8,56},{9,... | collective-permute-start | bytes 49160 | tf_op jit(solution)/shard_map/ppermute | solution.py:369
  158.4 5.8 %collective-permute-start.16 = (f32[32,128]{1,0:T(8,128)S(1)}, f32[32,128]{1,0:T(8,128)S(1)}, u32[]{:S(2)}, u32[]{:S(2)}) collective-permute-start(f32[32,128]{1,0:T(8,128)S(1)} %pad_maximum_fusion), channel_id=1, source_target_pairs={{0,56},{1,57},{2,58},{3,59},{4,60},{5,61},{6,62},{7,63},{8,48},{9,... | collective-permute-start | bytes 49160 | tf_op jit(solution)/shard_map/ppermute | solution.py:369

commit v3 on v2

--- a/solution.py
+++ b/solution.py
@@ -24,7 +24,7 @@
 ANY = pl.BlockSpec(memory_space=pl.ANY)
 
 
-def first_kernel(near, named, x_hbm, c_hbm, o_hbm, x, c, flat, out, x_sem, c_sem, o_sem):
+def first_kernel(place, near, named, x_hbm, c_hbm, o_hbm, x, c, flat, out, x_sem, c_sem, o_sem):
     tiles, count, rows, _ = c.shape
     slots, half = x.shape[1:]
     chunk = x.shape[0] // out.shape[0]
@@ -70,15 +70,19 @@
     for tile in range(tiles):
         store(tile).wait()
 
-
-def first_product(x, values, near, named, col_count):
+    @pl.when(place[0] == 1)
+    def _():
+        pl.delay(12000)
+
+
+def first_product(x, values, near, named, place, col_count):
     panel_rows, slots, half = x.shape
     tiles, count, rows, _ = values.shape
     chunk = panel_rows // col_count
     shape = (col_count, slots * chunk + 8, half)
     return pl.pallas_call(
         first_kernel,
-        in_specs=[SMEM, SMEM, ANY, ANY],
+        in_specs=[SMEM, SMEM, SMEM, ANY, ANY],
         out_specs=ANY,
         out_shape=pltpu.HBM(shape, jnp.bfloat16),
         scratch_shapes=[
@@ -93,7 +97,7 @@
         compiler_params=pltpu.CompilerParams(vmem_limit_bytes=60 << 20),
         cost_estimate=cost(2 * panel_rows * count * rows * slots * half, 6 << 20),
         name="first_product",
-    )(near, named, x, values)
+    )(place, near, named, x, values)
 
 
 def merge_kernel(x_ref, o_ref, ids_ref, total, ids, sem):
@@ -330,9 +334,9 @@
             x_ref[at, slot].astype(jnp.float32) * first * second_ref[pl.ds(lines[slot], 1), :]
             for slot in range(slots)
         ]
-        o_ref[part * chunk : (part + 1) * chunk] = jnp.swapaxes(jnp.stack(values), 0, 1).astype(
-            jnp.bfloat16
-        )
+        o_ref[part * chunk : (part + 1) * chunk] = jnp.concatenate(
+            [value.astype(jnp.bfloat16) for value in values], axis=1
+        ).reshape(chunk, slots, half)
 
 
 def final_scale(lines, x, first, second, parts):
@@ -405,7 +409,9 @@
     plan_width = float(slots * col_count * block_size)
 
     named = plan_blocks[0]
-    product = first_product(plan_values, first_values, first_blocks, named, col_count)
+    product = first_product(
+        plan_values, first_values, first_blocks, named, side.reshape(1), col_count
+    )
     arrived = lax.all_to_all(product, "col", split_axis=0, concat_axis=0, tiled=True)
     merged, ids = merge(arrived, col_count, blocks_here, chunk)
     merged, offset_first, offset_second = lax.optimization_barrier(
@@ -443,7 +449,7 @@
 
     chosen = select(ids, back, slots, half)
     home = lax.all_to_all(chosen, "col", split_axis=0, concat_axis=0, tiled=True)
-    new_plan = final_scale(lines, home, scale_first[:, None], all_second, 4)
+    new_plan = final_scale(lines, home, scale_first[:, None], all_second, 8)
     return (new_plan, scale_first, scale_second)
 
 

time: 168 us -> 160 us (0.952)
  blocking collectives: 66.8 us -> 51.4 us
  starting transfers between devices: 50.6 us -> 57.1 us
  waiting for transfers between devices: 22 us -> 23.7 us
    all_to_all x1, blocking collectives: 35.9 us -> 27.1 us  [local(): lax.all_to_all(product, 'col', split_axis=0, concat_axis=0, tiled=True)]
    ppermute x7, starting transfers between devices: 11.3 us -> 18.3 us  [swap(): return lax.ppermute(value, axis, [(i, i ^ bit) for i in range(size)])]
    all_to_all x1, blocking collectives: 30.9 us -> 24.3 us  [local(): lax.all_to_all(merged, 'col', split_axis=0, concat_axis=0, tiled=True)]
    ppermute x10, starting transfers between devices: 30.7 us -> 29 us  [move(): return lax.ppermute(value, ('row', 'col', 'pan'), pairs)]
where the time goes in v3:
time: 160 us; the launch traced here: 159 us
  starting transfers between devices  57.1 us (36%)
  blocking collectives  51.4 us (32%)
  Pallas kernels  24.6 us (15%)
  waiting for transfers between devices  23.7 us (15%)
    ppermute x10, starting transfers between devices, move(): return lax.ppermute(value, ('row', 'col', 'pan'), pairs)  29 us
    all_to_all x1, blocking collectives, local(): lax.all_to_all(product, 'col', split_axis=0, concat_axis=0, tiled=True)  27.1 us
    all_to_all x1, blocking collectives, local(): lax.all_to_all(merged, 'col', split_axis=0, concat_axis=0, tiled=True)  24.3 us
    ppermute x7, starting transfers between devices, swap(): return lax.ppermute(value, axis, [(i, i ^ bit) for i in range(size)])  18.3 us
    ppermute x10, waiting for transfers between devices, move(): return lax.ppermute(value, ('row', 'col', 'pan'), pairs)  13.2 us
    ppermute x7, waiting for transfers between devices, swap(): return lax.ppermute(value, axis, [(i, i ^ bit) for i in range(size)])  9.68 us
    all_to_all x1, starting transfers between devices, local(): lax.all_to_all(chosen, 'col', split_axis=0, concat_axis=0, tiled=True)  5.94 us
    pallas_call x1, Pallas kernels, first_product(): pl.pallas_call(first_kernel, in_specs=[SMEM, SMEM, SMEM, ANY, ANY], out_s...  5.92 us
  transfers between devices with their start and end apart: 19, of which 12 were waited for; matrix products, arithmetic and copies ran while one was open for 1% of the time, Pallas kernels for 4%

profile of v3, /device:TPU:32, one launch (start us, length us, event | category | flops | bytes accessed | tf_op | source)
XLA Modules:
  0.0 159.3 jit_solution(9311330169924798166)
XLA Ops:
  0.6 5.9 %first_product.1 = bf16[16,520,128]{2,1,0:T(8,128)(2,1)} custom-call(s32[1]{0:T(128)} %bitcast.1.place, s32[4,3]{1,0:T(4,128)} %near.2, s32[8]{0:T(128)} %bitcast.17, bf16[1024,8,128]{2,1,0:T(8,128)(2,1)} %x_hbm.1, bf16[4,3,256,256]{3,2,1,0:T(8,128)(2,1)} %c_hbm.1), custom_call_target="tpu_custom_call" | custom-call | flops 1610612736 | bytes 6291456 | tf_op jit(solution)/shard_map/first_product/pallas_call | solution.py:83
  6.6 27.1 %all_to_all.20.x_ref = bf16[16,520,128]{2,1,0:T(8,128)(2,1)S(1)} all-to-all(bf16[16,520,128]{2,1,0:T(8,128)(2,1)} %first_product.1), channel_id=1, replica_groups=mesh['row'=8,'col'=16,'pan'=2] {'col'}, dimensions={0} | all-to-all | bytes 4259840 | tf_op jit(solution)/shard_map/all_to_all | solution.py:415
  33.6 1.9 %merge.1 = (bf16[16,64,1024]{2,1,0:T(8,128)(2,1)S(1)}, s32[16,128]{1,0:T(8,128)S(1)}) custom-call(bf16[16,520,128]{2,1,0:T(8,128)(2,1)S(1)} %all_to_all.20.x_ref), custom_call_target="tpu_custom_call" | custom-call | bytes 8388608 | tf_op jit(solution)/shard_map/merge/pallas_call | solution.py:126
  35.6 24.3 %all_to_all.21.x_ref = bf16[16,64,1024]{2,1,0:T(8,128)(2,1)S(1)} all-to-all(bf16[16,64,1024]{2,1,0:T(8,128)(2,1)S(1)} %get-tuple-element.16), channel_id=1, replica_groups=mesh['row'=8,'col'=16,'pan'=2] {'col'}, dimensions={0} | all-to-all | bytes 4194304 | tf_op jit(solution)/shard_map/all_to_all | solution.py:420
  59.9 8.7 %collective-permute-start = (bf16[16,64,1024]{2,1,0:T(8,128)(2,1)S(1)}, bf16[16,64,1024]{2,1,0:T(8,128)(2,1)}, u32[]{:S(2)}, u32[]{:S(2)}) collective-permute-start(bf16[16,64,1024]{2,1,0:T(8,128)(2,1)S(1)} %all_to_all.21.x_ref), channel_id=1, source_target_pairs={{0,1},{1,0},{2,3},{3,2},{4,5},{5,4},{6,7},{7,6},{8,9},{9,8},{10,11... | collective-permute-start | bytes 6291464 | tf_op jit(solution)/shard_map/ppermute | solution.py:362
  68.6 0.1 reshape.32.ids
  68.7 0.2 copy.15.first_ref
  68.9 0.2 compare_reduce_fusion.1
  69.2 4.9 %second_near.1 = (f32[1024,1024]{1,0:T(8,128)S(1)}, bf16[1024,1024]{1,0:T(8,128)(2,1)S(1)}) custom-call(s32[8,6]{1,0:T(8,128)S(1)} %copy-done, s32[1]{0:T(128)} %bitcast.1.place, bf16[16,64,1024]{2,1,0:T(8,128)(2,1)S(1)} %all_to_all.21.x_ref, bf16[8,6,256,128]{3,2,1,0:T(8,128)(2,1)} %v_hbm.1), custom_call_target="tpu_custom_call" | custom-call | flops 2147483648 | bytes 8388608 | tf_op jit(solution)/shard_map/second_near/pallas_call | solution.py:214
  74.2 5.8 %second_far.1 = (bf16[16,64,1024]{2,1,0:T(8,128)(2,1)}, f32[2,1,512]{2,1,0:T(1,128)S(1)}) custom-call(bf16[16,64,1024]{2,1,0:T(8,128)(2,1)} %collective-permute-done.x_ref, bf16[1024,1024]{1,0:T(8,128)(2,1)S(1)} %get-tuple-element.17.m_ref, f32[1024,1024]{1,0:T(8,128)S(1)} %get-tuple-element.18.near_ref, f32[1024,1]{1,0:T(8,128)S(1)} %copy.15.first_ref, ...), custom_call_target="tpu_custom_call" | custom-call | flops 2147483648 | bytes 10485760 | tf_op jit(solution)/shard_map/second_far/pallas_call | solution.py:259
  80.0 3.9 %all-to-all-start.2 = ((bf16[16,64,1024]{2,1,0:T(8,128)(2,1)}), bf16[16,64,1024]{2,1,0:T(8,128)(2,1)S(1)}, u32[]{:S(2)}, u32[]{:S(2)}) async-start(bf16[16,64,1024]{2,1,0:T(8,128)(2,1)} %get-tuple-element.22.x_hbm), calls=%async_computation.2 | async-start | bytes 4194304 | tf_op jit(solution)/shard_map/all_to_all | solution.py:428
  83.9 0.1 collective-permute-start.1
  84.0 1.2 collective-permute-done.1
  85.1 1.9 %collective-permute-start.2 = (f32[8,128]{1,0:T(8,128)S(1)}, f32[8,128]{1,0:T(8,128)S(1)}, u32[]{:S(2)}, u32[]{:S(2)}) collective-permute-start(f32[8,128]{1,0:T(8,128)S(1)} %add.48), channel_id=1, source_target_pairs={{0,32},{1,35},{2,34},{3,33},{4,36},{5,39},{6,38},{7,37},{8,40},{9,... | collective-permute-start | bytes 12296 | tf_op jit(solution)/shard_map/ppermute | solution.py:373
  87.0 4.6 %collective-permute-start.3 = (f32[8,128]{1,0:T(8,128)S(1)}, f32[8,128]{1,0:T(8,128)S(1)}, u32[]{:S(2)}, u32[]{:S(2)}) collective-permute-start(f32[8,128]{1,0:T(8,128)S(1)} %add.48), channel_id=1, source_target_pairs={{0,36},{1,39},{2,38},{3,37},{4,32},{5,35},{6,34},{7,33},{8,44},{9,... | collective-permute-start | bytes 12296 | tf_op jit(solution)/shard_map/ppermute | solution.py:373
  91.6 1.6 collective-permute-done.3
  93.2 1.2 collective-permute-done.4
  94.4 2.2 %collective-permute-start.5 = (f32[8,128]{1,0:T(8,128)S(1)}, f32[8,128]{1,0:T(8,128)S(1)}, u32[]{:S(2)}, u32[]{:S(2)}) collective-permute-start(f32[8,128]{1,0:T(8,128)S(1)} %add.50), channel_id=1, source_target_pairs={{0,224},{1,233},{2,226},{3,235},{4,228},{5,237},{6,230},{7,239},{8... | collective-permute-start | bytes 12296 | tf_op jit(solution)/shard_map/ppermute | solution.py:373
  96.6 4.5 %collective-permute-start.6 = (f32[8,128]{1,0:T(8,128)S(1)}, f32[8,128]{1,0:T(8,128)S(1)}, u32[]{:S(2)}, u32[]{:S(2)}) collective-permute-start(f32[8,128]{1,0:T(8,128)S(1)} %add.50), channel_id=1, source_target_pairs={{0,240},{1,249},{2,242},{3,251},{4,244},{5,253},{6,246},{7,255},{8... | collective-permute-start | bytes 12296 | tf_op jit(solution)/shard_map/ppermute | solution.py:373
  101.1 3.1 %collective-permute-done.6 = f32[8,128]{1,0:T(8,128)S(1)} collective-permute-done((f32[8,128]{1,0:T(8,128)S(1)}, f32[8,128]{1,0:T(8,128)S(1)}, u32[]{:S(2)}, u32[]{:S(2)}) %collective-permute-start.6) | collective-permute-done | bytes 4128 | tf_op jit(solution)/shard_map/ppermute | solution.py:373
  104.2 0.1 pad.9.clone
  104.3 0.1 pad.5.clone
  104.4 1.0 collective-permute-done.7
  105.5 0.1 maximum_maximum_fusion.s_ref
  105.5 1.7 %weighted_colsum.1 = f32[8,128]{1,0:T(8,128)S(1)} custom-call(bf16[16,1024]{1,0:T(8,128)(2,1)S(1)} %maximum_maximum_fusion.s_ref, bf16[16,64,1024]{2,1,0:T(8,128)(2,1)} %get-tuple-element.22.x_hbm), custom_call_target="tpu_custom_call" | custom-call | flops 33554432 | bytes 4194304 | tf_op jit(solution)/shard_map/weighted_colsum/pallas_call | solution.py:313
  107.4 2.0 %collective-permute-start.8 = (f32[16,128]{1,0:T(8,128)S(1)}, f32[16,128]{1,0:T(8,128)S(1)}, u32[]{:S(2)}, u32[]{:S(2)}) collective-permute-start(f32[16,128]{1,0:T(8,128)S(1)} %pad_maximum_fusion.1), channel_id=1, source_target_pairs={{0,32},{32,0},{64,96},{96,64},{128,160},{160,128},{192,224},{224,1... | collective-permute-start | bytes 24584 | tf_op jit(solution)/shard_map/ppermute | solution.py:362
  109.4 1.7 %collective-permute-done.8 = f32[16,128]{1,0:T(8,128)S(1)} collective-permute-done((f32[16,128]{1,0:T(8,128)S(1)}, f32[16,128]{1,0:T(8,128)S(1)}, u32[]{:S(2)}, u32[]{:S(2)}) %collective-permute-start.8) | collective-permute-done | bytes 8224 | tf_op jit(solution)/shard_map/ppermute | solution.py:362
  111.1 3.8 %collective-permute-start.9 = (f32[16,128]{1,0:T(8,128)S(1)}, f32[16,128]{1,0:T(8,128)S(1)}, u32[]{:S(2)}, u32[]{:S(2)}) collective-permute-start(f32[16,128]{1,0:T(8,128)S(1)} %fusion.4), channel_id=1, source_target_pairs={{0,64},{32,96},{64,0},{96,32},{128,192},{160,224},{192,128},{224,1... | collective-permute-start | bytes 24584 | tf_op jit(solution)/shard_map/ppermute | solution.py:362
  114.9 1.6 %collective-permute-done.9 = f32[16,128]{1,0:T(8,128)S(1)} collective-permute-done((f32[16,128]{1,0:T(8,128)S(1)}, f32[16,128]{1,0:T(8,128)S(1)}, u32[]{:S(2)}, u32[]{:S(2)}) %collective-permute-start.9) | collective-permute-done | bytes 8224 | tf_op jit(solution)/shard_map/ppermute | solution.py:362
  116.5 0.9 all-to-all-done.2.x_ref
  117.4 2.0 %select.7 = bf16[16,8,64,128]{3,2,1,0:T(8,128)(2,1)} custom-call(s32[128]{0:T(128)S(1)} %reshape.32.ids, bf16[16,64,1024]{2,1,0:T(8,128)(2,1)S(1)} %all-to-all-done.2.x_ref), custom_call_target="tpu_custom_call" | custom-call | bytes 4194304 | tf_op jit(solution)/shard_map/select/pallas_call | solution.py:169
  119.5 5.9 %all-to-all-start.3 = ((bf16[16,8,64,128]{3,2,1,0:T(8,128)(2,1)}), bf16[16,8,64,128]{3,2,1,0:T(8,128)(2,1)S(1)}, u32[]{:S(2)}, u32[]{:S(2)}) async-start(bf16[16,8,64,128]{3,2,1,0:T(8,128)(2,1)} %select.7), calls=%async_computation.3 | async-start | bytes 4194304 | tf_op jit(solution)/shard_map/all_to_all | solution.py:451
  125.4 3.7 %collective-permute-start.10 = (f32[16,128]{1,0:T(8,128)S(1)}, f32[16,128]{1,0:T(8,128)S(1)}, u32[]{:S(2)}, u32[]{:S(2)}) collective-permute-start(f32[16,128]{1,0:T(8,128)S(1)} %add.54), channel_id=1, source_target_pairs={{0,224},{32,192},{64,160},{96,128},{128,96},{160,64},{192,32},{224... | collective-permute-start | bytes 24584 | tf_op jit(solution)/shard_map/ppermute | solution.py:362
  129.1 3.0 %collective-permute-done.10 = f32[16,128]{1,0:T(8,128)S(1)} collective-permute-done((f32[16,128]{1,0:T(8,128)S(1)}, f32[16,128]{1,0:T(8,128)S(1)}, u32[]{:S(2)}, u32[]{:S(2)}) %collective-permute-start.10) | collective-permute-done | bytes 8224 | tf_op jit(solution)/shard_map/ppermute | solution.py:362
  132.2 0.1 fusion.1
  132.3 0.1 compare_reduce_fusion
  132.4 0.1 constant_dynamic-update-slice_fusion.6
  132.5 2.8 %collective-permute-start.11 = (f32[8,128]{1,0:T(8,128)S(1)}, f32[8,128]{1,0:T(8,128)S(1)}, u32[]{:S(2)}, u32[]{:S(2)}) collective-permute-start(f32[8,128]{1,0:T(8,128)S(1)} %get-tuple-element.26), channel_id=1, source_target_pairs={{0,34},{1,35},{2,32},{3,33},{4,38},{5,39},{6,36},{7,37},{8,42},{9,... | collective-permute-start | bytes 12296 | tf_op jit(solution)/shard_map/ppermute | solution.py:373
  135.3 2.3 %collective-permute-start.12 = (f32[8,128]{1,0:T(8,128)S(1)}, f32[8,128]{1,0:T(8,128)S(1)}, u32[]{:S(2)}, u32[]{:S(2)}) collective-permute-start(f32[8,128]{1,0:T(8,128)S(1)} %get-tuple-element.26), channel_id=1, source_target_pairs={{0,36},{1,37},{2,38},{3,39},{4,32},{5,33},{6,34},{7,35},{8,44},{9,... | collective-permute-start | bytes 12296 | tf_op jit(solution)/shard_map/ppermute | solution.py:373
  137.6 1.5 collective-permute-start.13
  139.2 0.2 copy.16.first_ref
  139.4 2.0 %collective-permute-done.12 = f32[8,128]{1,0:T(8,128)S(1)} collective-permute-done((f32[8,128]{1,0:T(8,128)S(1)}, f32[8,128]{1,0:T(8,128)S(1)}, u32[]{:S(2)}, u32[]{:S(2)}) %collective-permute-start.12) | collective-permute-done | bytes 4128 | tf_op jit(solution)/shard_map/ppermute | solution.py:373
  141.4 2.0 %collective-permute-done.13 = f32[8,128]{1,0:T(8,128)S(1)} collective-permute-done((f32[8,128]{1,0:T(8,128)S(1)}, f32[8,128]{1,0:T(8,128)S(1)}, u32[]{:S(2)}, u32[]{:S(2)}) %collective-permute-start.13) | collective-permute-done | bytes 4128 | tf_op jit(solution)/shard_map/ppermute | solution.py:373
  143.4 2.8 %collective-permute-start.14 = (f32[32,128]{1,0:T(8,128)S(1)}, f32[32,128]{1,0:T(8,128)S(1)}, u32[]{:S(2)}, u32[]{:S(2)}) collective-permute-start(f32[32,128]{1,0:T(8,128)S(1)} %pad_maximum_fusion), channel_id=1, source_target_pairs={{0,40},{1,41},{2,42},{3,43},{4,44},{5,45},{6,46},{7,47},{8,32},{9,... | collective-permute-start | bytes 49160 | tf_op jit(solution)/shard_map/ppermute | solution.py:373
  146.2 5.0 %collective-permute-start.15 = (f32[32,128]{1,0:T(8,128)S(1)}, f32[32,128]{1,0:T(8,128)S(1)}, u32[]{:S(2)}, u32[]{:S(2)}) collective-permute-start(f32[32,128]{1,0:T(8,128)S(1)} %pad_maximum_fusion), channel_id=1, source_target_pairs={{0,48},{1,49},{2,50},{3,51},{4,52},{5,53},{6,54},{7,55},{8,56},{9,... | collective-permute-start | bytes 49160 | tf_op jit(solution)/shard_map/ppermute | solution.py:373
  151.2 1.4 collective-permute-start.16
  152.7 4.4 %collective-permute-done.16 = f32[32,128]{1,0:T(8,128)S(1)} collective-permute-done((f32[32,128]{1,0:T(8,128)S(1)}, f32[32,128]{1,0:T(8,128)S(1)}, u32[]{:S(2)}, u32[]{:S(2)}) %collective-permute-start.16) | collective-permute-done | bytes 16416 | tf_op jit(solution)/shard_map/ppermute | solution.py:373
  157.1 2.2 %final_scale.1 = bf16[1024,8,128]{2,1,0:T(8,128)(2,1)} custom-call(s32[8]{0:T(128)S(1)} %fusion.3.lines, bf16[16,8,64,128]{3,2,1,0:T(8,128)(2,1)S(1)} %all-to-all-done.3.x_ref, f32[1024,1]{1,0:T(8,128)S(1)} %copy.16.first_ref, f32[128,128]{1,0:T(8,128)S(1)} %constant_dynamic-update-slice_fusion.second_ref), custom_call_target="tpu_custom_call" | custom-call | bytes 5242880 | tf_op jit(solution)/shard_map/final_scale/pallas_call | solution.py:345
  (50 shorter events, 0.4 us)
Async XLA Ops:
  35.5 33.2 %copy-start.3 = (f32[1024]{0:T(1024)S(1)}, f32[1024]{0:T(1024)}, u32[]{:S(2)}) copy-start(f32[1024]{0:T(1024)} %param.18) | copy-start | bytes 12292
  35.5 33.6 %copy-start.5 = (f32[8,128]{1,0:T(8,128)S(1)}, f32[8,128]{1,0:T(8,128)}, u32[]{:S(2)}) copy-start(f32[8,128]{1,0:T(8,128)} %param.19) | copy-start | bytes 12292
  35.6 33.7 %copy-start = (s32[8,6]{1,0:T(8,128)S(1)}, s32[8,6]{1,0:T(8,128)}, u32[]{:S(2)}) copy-start(s32[8,6]{1,0:T(8,128)} %near.3) | copy-start | bytes 580
  59.9 14.3 %collective-permute-start = (bf16[16,64,1024]{2,1,0:T(8,128)(2,1)S(1)}, bf16[16,64,1024]{2,1,0:T(8,128)(2,1)}, u32[]{:S(2)}, u32[]{:S(2)}) collective-permute-start(bf16[16,64,1024]{2,1,0:T(8,128)(2,1)S(1)} %all_to_all.21.x_ref), channel_id=1, source_target_pairs={{0,1},{1,0},{2,3},{3,2},{4,5},{5,4},{6,7},{7,6},{8,9},{9,8},{10,11... | collective-permute-start | bytes 6291464 | tf_op jit(solution)/shard_map/ppermute | solution.py:362
  80.0 25.4 %copy-start.6 = (f32[1024]{0:T(1024)S(1)}, f32[1024]{0:T(1024)}, u32[]{:S(2)}) copy-start(f32[1024]{0:T(1024)} %param.16) | copy-start | bytes 12292
  80.0 37.4 %all-to-all-start.2 = ((bf16[16,64,1024]{2,1,0:T(8,128)(2,1)}), bf16[16,64,1024]{2,1,0:T(8,128)(2,1)S(1)}, u32[]{:S(2)}, u32[]{:S(2)}) async-start(bf16[16,64,1024]{2,1,0:T(8,128)(2,1)} %get-tuple-element.22.x_hbm), calls=%async_computation.2 | async-start | bytes 4194304 | tf_op jit(solution)/shard_map/all_to_all | solution.py:428
  83.9 1.3 collective-permute-start.1
  85.1 6.5 %collective-permute-start.2 = (f32[8,128]{1,0:T(8,128)S(1)}, f32[8,128]{1,0:T(8,128)S(1)}, u32[]{:S(2)}, u32[]{:S(2)}) collective-permute-start(f32[8,128]{1,0:T(8,128)S(1)} %add.48), channel_id=1, source_target_pairs={{0,32},{1,35},{2,34},{3,33},{4,36},{5,39},{6,38},{7,37},{8,40},{9,... | collective-permute-start | bytes 12296 | tf_op jit(solution)/shard_map/ppermute | solution.py:373
  87.0 6.2 %collective-permute-start.3 = (f32[8,128]{1,0:T(8,128)S(1)}, f32[8,128]{1,0:T(8,128)S(1)}, u32[]{:S(2)}, u32[]{:S(2)}) collective-permute-start(f32[8,128]{1,0:T(8,128)S(1)} %add.48), channel_id=1, source_target_pairs={{0,36},{1,39},{2,38},{3,37},{4,32},{5,35},{6,34},{7,33},{8,44},{9,... | collective-permute-start | bytes 12296 | tf_op jit(solution)/shard_map/ppermute | solution.py:373
  93.2 1.2 collective-permute-start.4
  94.4 6.7 %collective-permute-start.5 = (f32[8,128]{1,0:T(8,128)S(1)}, f32[8,128]{1,0:T(8,128)S(1)}, u32[]{:S(2)}, u32[]{:S(2)}) collective-permute-start(f32[8,128]{1,0:T(8,128)S(1)} %add.50), channel_id=1, source_target_pairs={{0,224},{1,233},{2,226},{3,235},{4,228},{5,237},{6,230},{7,239},{8... | collective-permute-start | bytes 12296 | tf_op jit(solution)/shard_map/ppermute | solution.py:373
  96.6 7.6 %collective-permute-start.6 = (f32[8,128]{1,0:T(8,128)S(1)}, f32[8,128]{1,0:T(8,128)S(1)}, u32[]{:S(2)}, u32[]{:S(2)}) collective-permute-start(f32[8,128]{1,0:T(8,128)S(1)} %add.50), channel_id=1, source_target_pairs={{0,240},{1,249},{2,242},{3,251},{4,244},{5,253},{6,246},{7,255},{8... | collective-permute-start | bytes 12296 | tf_op jit(solution)/shard_map/ppermute | solution.py:373
  104.2 1.2 collective-permute-start.7
  105.4 33.8 %copy-start.1 = (f32[1024]{0:T(1024)}, f32[1024]{0:T(1024)S(1)}, u32[]{:S(2)}) copy-start(f32[1024]{0:T(1024)S(1)} %get-tuple-element.28) | copy-start | bytes 12292
  107.4 3.7 %collective-permute-start.8 = (f32[16,128]{1,0:T(8,128)S(1)}, f32[16,128]{1,0:T(8,128)S(1)}, u32[]{:S(2)}, u32[]{:S(2)}) collective-permute-start(f32[16,128]{1,0:T(8,128)S(1)} %pad_maximum_fusion.1), channel_id=1, source_target_pairs={{0,32},{32,0},{64,96},{96,64},{128,160},{160,128},{192,224},{224,1... | collective-permute-start | bytes 24584 | tf_op jit(solution)/shard_map/ppermute | solution.py:362
  111.1 5.4 %collective-permute-start.9 = (f32[16,128]{1,0:T(8,128)S(1)}, f32[16,128]{1,0:T(8,128)S(1)}, u32[]{:S(2)}, u32[]{:S(2)}) collective-permute-start(f32[16,128]{1,0:T(8,128)S(1)} %fusion.4), channel_id=1, source_target_pairs={{0,64},{32,96},{64,0},{96,32},{128,192},{160,224},{192,128},{224,1... | collective-permute-start | bytes 24584 | tf_op jit(solution)/shard_map/ppermute | solution.py:362
  119.5 13.0 %copy-start.4 = (f32[8,128]{1,0:T(8,128)S(1)}, f32[8,128]{1,0:T(8,128)}, u32[]{:S(2)}) copy-start(f32[8,128]{1,0:T(8,128)} %param.17) | copy-start | bytes 12292
  119.5 19.7 %copy-start.7 = (s32[1,8]{1,0:T(1,128)S(1)}, s32[1,8]{1,0:T(1,128)}, u32[]{:S(2)}) copy-start(s32[1,8]{1,0:T(1,128)} %param.11) | copy-start | bytes 100
  119.5 37.6 %all-to-all-start.3 = ((bf16[16,8,64,128]{3,2,1,0:T(8,128)(2,1)}), bf16[16,8,64,128]{3,2,1,0:T(8,128)(2,1)S(1)}, u32[]{:S(2)}, u32[]{:S(2)}) async-start(bf16[16,8,64,128]{3,2,1,0:T(8,128)(2,1)} %select.7), calls=%async_computation.3 | async-start | bytes 4194304 | tf_op jit(solution)/shard_map/all_to_all | solution.py:451
  125.4 6.7 %collective-permute-start.10 = (f32[16,128]{1,0:T(8,128)S(1)}, f32[16,128]{1,0:T(8,128)S(1)}, u32[]{:S(2)}, u32[]{:S(2)}) collective-permute-start(f32[16,128]{1,0:T(8,128)S(1)} %add.54), channel_id=1, source_target_pairs={{0,224},{32,192},{64,160},{96,128},{128,96},{160,64},{192,32},{224... | collective-permute-start | bytes 24584 | tf_op jit(solution)/shard_map/ppermute | solution.py:362
  132.5 26.8 %copy-start.2 = (f32[8,128]{1,0:T(8,128)}, f32[8,128]{1,0:T(8,128)S(1)}, u32[]{:S(2)}) copy-start(f32[8,128]{1,0:T(8,128)S(1)} %get-tuple-element.26) | copy-start | bytes 12292
  132.5 6.9 %collective-permute-start.11 = (f32[8,128]{1,0:T(8,128)S(1)}, f32[8,128]{1,0:T(8,128)S(1)}, u32[]{:S(2)}, u32[]{:S(2)}) collective-permute-start(f32[8,128]{1,0:T(8,128)S(1)} %get-tuple-element.26), channel_id=1, source_target_pairs={{0,34},{1,35},{2,32},{3,33},{4,38},{5,39},{6,36},{7,37},{8,42},{9,... | collective-permute-start | bytes 12296 | tf_op jit(solution)/shard_map/ppermute | solution.py:373
  135.3 6.1 %collective-permute-start.12 = (f32[8,128]{1,0:T(8,128)S(1)}, f32[8,128]{1,0:T(8,128)S(1)}, u32[]{:S(2)}, u32[]{:S(2)}) collective-permute-start(f32[8,128]{1,0:T(8,128)S(1)} %get-tuple-element.26), channel_id=1, source_target_pairs={{0,36},{1,37},{2,38},{3,39},{4,32},{5,33},{6,34},{7,35},{8,44},{9,... | collective-permute-start | bytes 12296 | tf_op jit(solution)/shard_map/ppermute | solution.py:373
  137.6 5.8 %collective-permute-start.13 = (f32[8,128]{1,0:T(8,128)S(1)}, f32[8,128]{1,0:T(8,128)S(1)}, u32[]{:S(2)}, u32[]{:S(2)}) collective-permute-start(f32[8,128]{1,0:T(8,128)S(1)} %get-tuple-element.26), channel_id=1, source_target_pairs={{0,38},{1,39},{2,36},{3,37},{4,34},{5,35},{6,32},{7,33},{8,46},{9,... | collective-permute-start | bytes 12296 | tf_op jit(solution)/shard_map/ppermute | solution.py:373
  143.4 9.2 %collective-permute-start.14 = (f32[32,128]{1,0:T(8,128)S(1)}, f32[32,128]{1,0:T(8,128)S(1)}, u32[]{:S(2)}, u32[]{:S(2)}) collective-permute-start(f32[32,128]{1,0:T(8,128)S(1)} %pad_maximum_fusion), channel_id=1, source_target_pairs={{0,40},{1,41},{2,42},{3,43},{4,44},{5,45},{6,46},{7,47},{8,32},{9,... | collective-permute-start | bytes 49160 | tf_op jit(solution)/shard_map/ppermute | solution.py:373
  146.2 6.4 %collective-permute-start.15 = (f32[32,128]{1,0:T(8,128)S(1)}, f32[32,128]{1,0:T(8,128)S(1)}, u32[]{:S(2)}, u32[]{:S(2)}) collective-permute-start(f32[32,128]{1,0:T(8,128)S(1)} %pad_maximum_fusion), channel_id=1, source_target_pairs={{0,48},{1,49},{2,50},{3,51},{4,52},{5,53},{6,54},{7,55},{8,56},{9,... | collective-permute-start | bytes 49160 | tf_op jit(solution)/shard_map/ppermute | solution.py:373
  151.2 5.8 %collective-permute-start.16 = (f32[32,128]{1,0:T(8,128)S(1)}, f32[32,128]{1,0:T(8,128)S(1)}, u32[]{:S(2)}, u32[]{:S(2)}) collective-permute-start(f32[32,128]{1,0:T(8,128)S(1)} %pad_maximum_fusion), channel_id=1, source_target_pairs={{0,56},{1,57},{2,58},{3,59},{4,60},{5,61},{6,62},{7,63},{8,48},{9,... | collective-permute-start | bytes 49160 | tf_op jit(solution)/shard_map/ppermute | solution.py:373

commit v4 on v3

--- a/solution.py
+++ b/solution.py
@@ -72,7 +72,7 @@
 
     @pl.when(place[0] == 1)
     def _():
-        pl.delay(12000)
+        pl.delay(14000)
 
 
 def first_product(x, values, near, named, place, col_count):

time: 160 us -> 159 us (level)
  blocking collectives: 51.4 us -> 48.4 us
  starting transfers between devices: 57.1 us -> 59.2 us
    ppermute x7, starting transfers between devices: 18.3 us -> 20.4 us  [swap(): return lax.ppermute(value, axis, [(i, i ^ bit) for i in range(size)])]
    all_to_all x1, blocking collectives: 24.3 us -> 22.3 us  [local(): lax.all_to_all(merged, 'col', split_axis=0, concat_axis=0, tiled=True)]
where the time goes in v4:
time: 159 us; the launch traced here: 158 us
  starting transfers between devices  59.2 us (37%)
  blocking collectives  48.4 us (30%)
  Pallas kernels  24.6 us (15%)
  waiting for transfers between devices  23.7 us (15%)
    ppermute x10, starting transfers between devices, move(): return lax.ppermute(value, ('row', 'col', 'pan'), pairs)  29.1 us
    all_to_all x1, blocking collectives, local(): lax.all_to_all(product, 'col', split_axis=0, concat_axis=0, tiled=True)  26.1 us
    all_to_all x1, blocking collectives, local(): lax.all_to_all(merged, 'col', split_axis=0, concat_axis=0, tiled=True)  22.3 us
    ppermute x7, starting transfers between devices, swap(): return lax.ppermute(value, axis, [(i, i ^ bit) for i in range(size)])  20.4 us
    ppermute x10, waiting for transfers between devices, move(): return lax.ppermute(value, ('row', 'col', 'pan'), pairs)  13.1 us
    ppermute x7, waiting for transfers between devices, swap(): return lax.ppermute(value, axis, [(i, i ^ bit) for i in range(size)])  9.67 us
    all_to_all x1, starting transfers between devices, local(): lax.all_to_all(chosen, 'col', split_axis=0, concat_axis=0, tiled=True)  5.93 us
    pallas_call x1, Pallas kernels, first_product(): pl.pallas_call(first_kernel, in_specs=[SMEM, SMEM, SMEM, ANY, ANY], out_s...  5.92 us
  transfers between devices with their start and end apart: 19, of which 12 were waited for; matrix products, arithmetic and copies ran while one was open for 1% of the time, Pallas kernels for 4%

profile of v4, /device:TPU:32, one launch (start us, length us, event | category | flops | bytes accessed | tf_op | source)
XLA Modules:
  0.0 158.4 jit_solution(10687097084493387507)
XLA Ops:
  0.6 5.9 %first_product.1 = bf16[16,520,128]{2,1,0:T(8,128)(2,1)} custom-call(s32[1]{0:T(128)} %bitcast.1.place, s32[4,3]{1,0:T(4,128)} %near.2, s32[8]{0:T(128)} %bitcast.17, bf16[1024,8,128]{2,1,0:T(8,128)(2,1)} %x_hbm.1, bf16[4,3,256,256]{3,2,1,0:T(8,128)(2,1)} %c_hbm.1), custom_call_target="tpu_custom_call" | custom-call | flops 1610612736 | bytes 6291456 | tf_op jit(solution)/shard_map/first_product/pallas_call | solution.py:83
  6.6 26.1 %all_to_all.20.x_ref = bf16[16,520,128]{2,1,0:T(8,128)(2,1)S(1)} all-to-all(bf16[16,520,128]{2,1,0:T(8,128)(2,1)} %first_product.1), channel_id=1, replica_groups=mesh['row'=8,'col'=16,'pan'=2] {'col'}, dimensions={0} | all-to-all | bytes 4259840 | tf_op jit(solution)/shard_map/all_to_all | solution.py:415
  32.6 1.9 %merge.1 = (bf16[16,64,1024]{2,1,0:T(8,128)(2,1)S(1)}, s32[16,128]{1,0:T(8,128)S(1)}) custom-call(bf16[16,520,128]{2,1,0:T(8,128)(2,1)S(1)} %all_to_all.20.x_ref), custom_call_target="tpu_custom_call" | custom-call | bytes 8388608 | tf_op jit(solution)/shard_map/merge/pallas_call | solution.py:126
  34.6 22.3 %all_to_all.21.x_ref = bf16[16,64,1024]{2,1,0:T(8,128)(2,1)S(1)} all-to-all(bf16[16,64,1024]{2,1,0:T(8,128)(2,1)S(1)} %get-tuple-element.16), channel_id=1, replica_groups=mesh['row'=8,'col'=16,'pan'=2] {'col'}, dimensions={0} | all-to-all | bytes 4194304 | tf_op jit(solution)/shard_map/all_to_all | solution.py:420
  56.9 10.8 %collective-permute-start = (bf16[16,64,1024]{2,1,0:T(8,128)(2,1)S(1)}, bf16[16,64,1024]{2,1,0:T(8,128)(2,1)}, u32[]{:S(2)}, u32[]{:S(2)}) collective-permute-start(bf16[16,64,1024]{2,1,0:T(8,128)(2,1)S(1)} %all_to_all.21.x_ref), channel_id=1, source_target_pairs={{0,1},{1,0},{2,3},{3,2},{4,5},{5,4},{6,7},{7,6},{8,9},{9,8},{10,11... | collective-permute-start | bytes 6291464 | tf_op jit(solution)/shard_map/ppermute | solution.py:362
  67.7 0.1 reshape.32.ids
  67.8 0.2 copy.15.first_ref
  68.0 0.2 compare_reduce_fusion.1
  68.3 4.9 %second_near.1 = (f32[1024,1024]{1,0:T(8,128)S(1)}, bf16[1024,1024]{1,0:T(8,128)(2,1)S(1)}) custom-call(s32[8,6]{1,0:T(8,128)S(1)} %copy-done, s32[1]{0:T(128)} %bitcast.1.place, bf16[16,64,1024]{2,1,0:T(8,128)(2,1)S(1)} %all_to_all.21.x_ref, bf16[8,6,256,128]{3,2,1,0:T(8,128)(2,1)} %v_hbm.1), custom_call_target="tpu_custom_call" | custom-call | flops 2147483648 | bytes 8388608 | tf_op jit(solution)/shard_map/second_near/pallas_call | solution.py:214
  73.2 5.8 %second_far.1 = (bf16[16,64,1024]{2,1,0:T(8,128)(2,1)}, f32[2,1,512]{2,1,0:T(1,128)S(1)}) custom-call(bf16[16,64,1024]{2,1,0:T(8,128)(2,1)} %collective-permute-done.x_ref, bf16[1024,1024]{1,0:T(8,128)(2,1)S(1)} %get-tuple-element.17.m_ref, f32[1024,1024]{1,0:T(8,128)S(1)} %get-tuple-element.18.near_ref, f32[1024,1]{1,0:T(8,128)S(1)} %copy.15.first_ref, ...), custom_call_target="tpu_custom_call" | custom-call | flops 2147483648 | bytes 10485760 | tf_op jit(solution)/shard_map/second_far/pallas_call | solution.py:259
  79.1 3.9 %all-to-all-start.2 = ((bf16[16,64,1024]{2,1,0:T(8,128)(2,1)}), bf16[16,64,1024]{2,1,0:T(8,128)(2,1)S(1)}, u32[]{:S(2)}, u32[]{:S(2)}) async-start(bf16[16,64,1024]{2,1,0:T(8,128)(2,1)} %get-tuple-element.22.x_hbm), calls=%async_computation.2 | async-start | bytes 4194304 | tf_op jit(solution)/shard_map/all_to_all | solution.py:428
  82.9 0.1 collective-permute-start.1
  83.0 1.2 collective-permute-done.1
  84.2 1.9 %collective-permute-start.2 = (f32[8,128]{1,0:T(8,128)S(1)}, f32[8,128]{1,0:T(8,128)S(1)}, u32[]{:S(2)}, u32[]{:S(2)}) collective-permute-start(f32[8,128]{1,0:T(8,128)S(1)} %add.48), channel_id=1, source_target_pairs={{0,32},{1,35},{2,34},{3,33},{4,36},{5,39},{6,38},{7,37},{8,40},{9,... | collective-permute-start | bytes 12296 | tf_op jit(solution)/shard_map/ppermute | solution.py:373
  86.1 4.6 %collective-permute-start.3 = (f32[8,128]{1,0:T(8,128)S(1)}, f32[8,128]{1,0:T(8,128)S(1)}, u32[]{:S(2)}, u32[]{:S(2)}) collective-permute-start(f32[8,128]{1,0:T(8,128)S(1)} %add.48), channel_id=1, source_target_pairs={{0,36},{1,39},{2,38},{3,37},{4,32},{5,35},{6,34},{7,33},{8,44},{9,... | collective-permute-start | bytes 12296 | tf_op jit(solution)/shard_map/ppermute | solution.py:373
  90.7 1.6 collective-permute-done.3
  92.3 1.2 collective-permute-done.4
  93.4 2.2 %collective-permute-start.5 = (f32[8,128]{1,0:T(8,128)S(1)}, f32[8,128]{1,0:T(8,128)S(1)}, u32[]{:S(2)}, u32[]{:S(2)}) collective-permute-start(f32[8,128]{1,0:T(8,128)S(1)} %add.50), channel_id=1, source_target_pairs={{0,224},{1,233},{2,226},{3,235},{4,228},{5,237},{6,230},{7,239},{8... | collective-permute-start | bytes 12296 | tf_op jit(solution)/shard_map/ppermute | solution.py:373
  95.7 4.5 %collective-permute-start.6 = (f32[8,128]{1,0:T(8,128)S(1)}, f32[8,128]{1,0:T(8,128)S(1)}, u32[]{:S(2)}, u32[]{:S(2)}) collective-permute-start(f32[8,128]{1,0:T(8,128)S(1)} %add.50), channel_id=1, source_target_pairs={{0,240},{1,249},{2,242},{3,251},{4,244},{5,253},{6,246},{7,255},{8... | collective-permute-start | bytes 12296 | tf_op jit(solution)/shard_map/ppermute | solution.py:373
  100.2 3.1 %collective-permute-done.6 = f32[8,128]{1,0:T(8,128)S(1)} collective-permute-done((f32[8,128]{1,0:T(8,128)S(1)}, f32[8,128]{1,0:T(8,128)S(1)}, u32[]{:S(2)}, u32[]{:S(2)}) %collective-permute-start.6) | collective-permute-done | bytes 4128 | tf_op jit(solution)/shard_map/ppermute | solution.py:373
  103.3 0.1 pad.9.clone
  103.4 0.1 pad.5.clone
  103.5 1.0 collective-permute-done.7
  104.5 0.1 maximum_maximum_fusion.s_ref
  104.6 1.7 %weighted_colsum.1 = f32[8,128]{1,0:T(8,128)S(1)} custom-call(bf16[16,1024]{1,0:T(8,128)(2,1)S(1)} %maximum_maximum_fusion.s_ref, bf16[16,64,1024]{2,1,0:T(8,128)(2,1)} %get-tuple-element.22.x_hbm), custom_call_target="tpu_custom_call" | custom-call | flops 33554432 | bytes 4194304 | tf_op jit(solution)/shard_map/weighted_colsum/pallas_call | solution.py:313
  106.4 2.0 %collective-permute-start.8 = (f32[16,128]{1,0:T(8,128)S(1)}, f32[16,128]{1,0:T(8,128)S(1)}, u32[]{:S(2)}, u32[]{:S(2)}) collective-permute-start(f32[16,128]{1,0:T(8,128)S(1)} %pad_maximum_fusion.1), channel_id=1, source_target_pairs={{0,32},{32,0},{64,96},{96,64},{128,160},{160,128},{192,224},{224,1... | collective-permute-start | bytes 24584 | tf_op jit(solution)/shard_map/ppermute | solution.py:362
  108.4 1.7 %collective-permute-done.8 = f32[16,128]{1,0:T(8,128)S(1)} collective-permute-done((f32[16,128]{1,0:T(8,128)S(1)}, f32[16,128]{1,0:T(8,128)S(1)}, u32[]{:S(2)}, u32[]{:S(2)}) %collective-permute-start.8) | collective-permute-done | bytes 8224 | tf_op jit(solution)/shard_map/ppermute | solution.py:362
  110.2 3.8 %collective-permute-start.9 = (f32[16,128]{1,0:T(8,128)S(1)}, f32[16,128]{1,0:T(8,128)S(1)}, u32[]{:S(2)}, u32[]{:S(2)}) collective-permute-start(f32[16,128]{1,0:T(8,128)S(1)} %fusion.4), channel_id=1, source_target_pairs={{0,64},{32,96},{64,0},{96,32},{128,192},{160,224},{192,128},{224,1... | collective-permute-start | bytes 24584 | tf_op jit(solution)/shard_map/ppermute | solution.py:362
  114.0 1.6 %collective-permute-done.9 = f32[16,128]{1,0:T(8,128)S(1)} collective-permute-done((f32[16,128]{1,0:T(8,128)S(1)}, f32[16,128]{1,0:T(8,128)S(1)}, u32[]{:S(2)}, u32[]{:S(2)}) %collective-permute-start.9) | collective-permute-done | bytes 8224 | tf_op jit(solution)/shard_map/ppermute | solution.py:362
  115.6 0.9 all-to-all-done.2.x_ref
  116.5 2.0 %select.7 = bf16[16,8,64,128]{3,2,1,0:T(8,128)(2,1)} custom-call(s32[128]{0:T(128)S(1)} %reshape.32.ids, bf16[16,64,1024]{2,1,0:T(8,128)(2,1)S(1)} %all-to-all-done.2.x_ref), custom_call_target="tpu_custom_call" | custom-call | bytes 4194304 | tf_op jit(solution)/shard_map/select/pallas_call | solution.py:169
  118.6 5.9 %all-to-all-start.3 = ((bf16[16,8,64,128]{3,2,1,0:T(8,128)(2,1)}), bf16[16,8,64,128]{3,2,1,0:T(8,128)(2,1)S(1)}, u32[]{:S(2)}, u32[]{:S(2)}) async-start(bf16[16,8,64,128]{3,2,1,0:T(8,128)(2,1)} %select.7), calls=%async_computation.3 | async-start | bytes 4194304 | tf_op jit(solution)/shard_map/all_to_all | solution.py:451
  124.5 3.7 %collective-permute-start.10 = (f32[16,128]{1,0:T(8,128)S(1)}, f32[16,128]{1,0:T(8,128)S(1)}, u32[]{:S(2)}, u32[]{:S(2)}) collective-permute-start(f32[16,128]{1,0:T(8,128)S(1)} %add.54), channel_id=1, source_target_pairs={{0,224},{32,192},{64,160},{96,128},{128,96},{160,64},{192,32},{224... | collective-permute-start | bytes 24584 | tf_op jit(solution)/shard_map/ppermute | solution.py:362
  128.2 3.0 %collective-permute-done.10 = f32[16,128]{1,0:T(8,128)S(1)} collective-permute-done((f32[16,128]{1,0:T(8,128)S(1)}, f32[16,128]{1,0:T(8,128)S(1)}, u32[]{:S(2)}, u32[]{:S(2)}) %collective-permute-start.10) | collective-permute-done | bytes 8224 | tf_op jit(solution)/shard_map/ppermute | solution.py:362
  131.3 0.1 fusion.1
  131.4 0.1 compare_reduce_fusion
  131.5 0.1 constant_dynamic-update-slice_fusion.6
  131.6 2.8 %collective-permute-start.11 = (f32[8,128]{1,0:T(8,128)S(1)}, f32[8,128]{1,0:T(8,128)S(1)}, u32[]{:S(2)}, u32[]{:S(2)}) collective-permute-start(f32[8,128]{1,0:T(8,128)S(1)} %get-tuple-element.26), channel_id=1, source_target_pairs={{0,34},{1,35},{2,32},{3,33},{4,38},{5,39},{6,36},{7,37},{8,42},{9,... | collective-permute-start | bytes 12296 | tf_op jit(solution)/shard_map/ppermute | solution.py:373
  134.4 2.3 %collective-permute-start.12 = (f32[8,128]{1,0:T(8,128)S(1)}, f32[8,128]{1,0:T(8,128)S(1)}, u32[]{:S(2)}, u32[]{:S(2)}) collective-permute-start(f32[8,128]{1,0:T(8,128)S(1)} %get-tuple-element.26), channel_id=1, source_target_pairs={{0,36},{1,37},{2,38},{3,39},{4,32},{5,33},{6,34},{7,35},{8,44},{9,... | collective-permute-start | bytes 12296 | tf_op jit(solution)/shard_map/ppermute | solution.py:373
  136.7 1.5 collective-permute-start.13
  138.3 0.2 copy.16.first_ref
  138.5 2.0 %collective-permute-done.12 = f32[8,128]{1,0:T(8,128)S(1)} collective-permute-done((f32[8,128]{1,0:T(8,128)S(1)}, f32[8,128]{1,0:T(8,128)S(1)}, u32[]{:S(2)}, u32[]{:S(2)}) %collective-permute-start.12) | collective-permute-done | bytes 4128 | tf_op jit(solution)/shard_map/ppermute | solution.py:373
  140.5 2.0 %collective-permute-done.13 = f32[8,128]{1,0:T(8,128)S(1)} collective-permute-done((f32[8,128]{1,0:T(8,128)S(1)}, f32[8,128]{1,0:T(8,128)S(1)}, u32[]{:S(2)}, u32[]{:S(2)}) %collective-permute-start.13) | collective-permute-done | bytes 4128 | tf_op jit(solution)/shard_map/ppermute | solution.py:373
  142.5 2.8 %collective-permute-start.14 = (f32[32,128]{1,0:T(8,128)S(1)}, f32[32,128]{1,0:T(8,128)S(1)}, u32[]{:S(2)}, u32[]{:S(2)}) collective-permute-start(f32[32,128]{1,0:T(8,128)S(1)} %pad_maximum_fusion), channel_id=1, source_target_pairs={{0,40},{1,41},{2,42},{3,43},{4,44},{5,45},{6,46},{7,47},{8,32},{9,... | collective-permute-start | bytes 49160 | tf_op jit(solution)/shard_map/ppermute | solution.py:373
  145.3 5.0 %collective-permute-start.15 = (f32[32,128]{1,0:T(8,128)S(1)}, f32[32,128]{1,0:T(8,128)S(1)}, u32[]{:S(2)}, u32[]{:S(2)}) collective-permute-start(f32[32,128]{1,0:T(8,128)S(1)} %pad_maximum_fusion), channel_id=1, source_target_pairs={{0,48},{1,49},{2,50},{3,51},{4,52},{5,53},{6,54},{7,55},{8,56},{9,... | collective-permute-start | bytes 49160 | tf_op jit(solution)/shard_map/ppermute | solution.py:373
  150.3 1.4 collective-permute-start.16
  151.8 4.4 %collective-permute-done.16 = f32[32,128]{1,0:T(8,128)S(1)} collective-permute-done((f32[32,128]{1,0:T(8,128)S(1)}, f32[32,128]{1,0:T(8,128)S(1)}, u32[]{:S(2)}, u32[]{:S(2)}) %collective-permute-start.16) | collective-permute-done | bytes 16416 | tf_op jit(solution)/shard_map/ppermute | solution.py:373
  156.2 2.2 %final_scale.1 = bf16[1024,8,128]{2,1,0:T(8,128)(2,1)} custom-call(s32[8]{0:T(128)S(1)} %fusion.3.lines, bf16[16,8,64,128]{3,2,1,0:T(8,128)(2,1)S(1)} %all-to-all-done.3.x_ref, f32[1024,1]{1,0:T(8,128)S(1)} %copy.16.first_ref, f32[128,128]{1,0:T(8,128)S(1)} %constant_dynamic-update-slice_fusion.second_ref), custom_call_target="tpu_custom_call" | custom-call | bytes 5242880 | tf_op jit(solution)/shard_map/final_scale/pallas_call | solution.py:345
  (50 shorter events, 0.4 us)
Async XLA Ops:
  34.5 33.2 %copy-start.3 = (f32[1024]{0:T(1024)S(1)}, f32[1024]{0:T(1024)}, u32[]{:S(2)}) copy-start(f32[1024]{0:T(1024)} %param.18) | copy-start | bytes 12292
  34.6 33.6 %copy-start.5 = (f32[8,128]{1,0:T(8,128)S(1)}, f32[8,128]{1,0:T(8,128)}, u32[]{:S(2)}) copy-start(f32[8,128]{1,0:T(8,128)} %param.19) | copy-start | bytes 12292
  34.6 33.7 %copy-start = (s32[8,6]{1,0:T(8,128)S(1)}, s32[8,6]{1,0:T(8,128)}, u32[]{:S(2)}) copy-start(s32[8,6]{1,0:T(8,128)} %near.3) | copy-start | bytes 580
  56.9 16.4 %collective-permute-start = (bf16[16,64,1024]{2,1,0:T(8,128)(2,1)S(1)}, bf16[16,64,1024]{2,1,0:T(8,128)(2,1)}, u32[]{:S(2)}, u32[]{:S(2)}) collective-permute-start(bf16[16,64,1024]{2,1,0:T(8,128)(2,1)S(1)} %all_to_all.21.x_ref), channel_id=1, source_target_pairs={{0,1},{1,0},{2,3},{3,2},{4,5},{5,4},{6,7},{7,6},{8,9},{9,8},{10,11... | collective-permute-start | bytes 6291464 | tf_op jit(solution)/shard_map/ppermute | solution.py:362
  79.1 25.4 %copy-start.6 = (f32[1024]{0:T(1024)S(1)}, f32[1024]{0:T(1024)}, u32[]{:S(2)}) copy-start(f32[1024]{0:T(1024)} %param.16) | copy-start | bytes 12292
  79.1 37.4 %all-to-all-start.2 = ((bf16[16,64,1024]{2,1,0:T(8,128)(2,1)}), bf16[16,64,1024]{2,1,0:T(8,128)(2,1)S(1)}, u32[]{:S(2)}, u32[]{:S(2)}) async-start(bf16[16,64,1024]{2,1,0:T(8,128)(2,1)} %get-tuple-element.22.x_hbm), calls=%async_computation.2 | async-start | bytes 4194304 | tf_op jit(solution)/shard_map/all_to_all | solution.py:428
  82.9 1.3 collective-permute-start.1
  84.2 6.5 %collective-permute-start.2 = (f32[8,128]{1,0:T(8,128)S(1)}, f32[8,128]{1,0:T(8,128)S(1)}, u32[]{:S(2)}, u32[]{:S(2)}) collective-permute-start(f32[8,128]{1,0:T(8,128)S(1)} %add.48), channel_id=1, source_target_pairs={{0,32},{1,35},{2,34},{3,33},{4,36},{5,39},{6,38},{7,37},{8,40},{9,... | collective-permute-start | bytes 12296 | tf_op jit(solution)/shard_map/ppermute | solution.py:373
  86.1 6.2 %collective-permute-start.3 = (f32[8,128]{1,0:T(8,128)S(1)}, f32[8,128]{1,0:T(8,128)S(1)}, u32[]{:S(2)}, u32[]{:S(2)}) collective-permute-start(f32[8,128]{1,0:T(8,128)S(1)} %add.48), channel_id=1, source_target_pairs={{0,36},{1,39},{2,38},{3,37},{4,32},{5,35},{6,34},{7,33},{8,44},{9,... | collective-permute-start | bytes 12296 | tf_op jit(solution)/shard_map/ppermute | solution.py:373
  92.3 1.2 collective-permute-start.4
  93.4 6.7 %collective-permute-start.5 = (f32[8,128]{1,0:T(8,128)S(1)}, f32[8,128]{1,0:T(8,128)S(1)}, u32[]{:S(2)}, u32[]{:S(2)}) collective-permute-start(f32[8,128]{1,0:T(8,128)S(1)} %add.50), channel_id=1, source_target_pairs={{0,224},{1,233},{2,226},{3,235},{4,228},{5,237},{6,230},{7,239},{8... | collective-permute-start | bytes 12296 | tf_op jit(solution)/shard_map/ppermute | solution.py:373
  95.7 7.6 %collective-permute-start.6 = (f32[8,128]{1,0:T(8,128)S(1)}, f32[8,128]{1,0:T(8,128)S(1)}, u32[]{:S(2)}, u32[]{:S(2)}) collective-permute-start(f32[8,128]{1,0:T(8,128)S(1)} %add.50), channel_id=1, source_target_pairs={{0,240},{1,249},{2,242},{3,251},{4,244},{5,253},{6,246},{7,255},{8... | collective-permute-start | bytes 12296 | tf_op jit(solution)/shard_map/ppermute | solution.py:373
  103.3 1.2 collective-permute-start.7
  104.5 33.8 %copy-start.1 = (f32[1024]{0:T(1024)}, f32[1024]{0:T(1024)S(1)}, u32[]{:S(2)}) copy-start(f32[1024]{0:T(1024)S(1)} %get-tuple-element.28) | copy-start | bytes 12292
  106.4 3.7 %collective-permute-start.8 = (f32[16,128]{1,0:T(8,128)S(1)}, f32[16,128]{1,0:T(8,128)S(1)}, u32[]{:S(2)}, u32[]{:S(2)}) collective-permute-start(f32[16,128]{1,0:T(8,128)S(1)} %pad_maximum_fusion.1), channel_id=1, source_target_pairs={{0,32},{32,0},{64,96},{96,64},{128,160},{160,128},{192,224},{224,1... | collective-permute-start | bytes 24584 | tf_op jit(solution)/shard_map/ppermute | solution.py:362
  110.2 5.4 %collective-permute-start.9 = (f32[16,128]{1,0:T(8,128)S(1)}, f32[16,128]{1,0:T(8,128)S(1)}, u32[]{:S(2)}, u32[]{:S(2)}) collective-permute-start(f32[16,128]{1,0:T(8,128)S(1)} %fusion.4), channel_id=1, source_target_pairs={{0,64},{32,96},{64,0},{96,32},{128,192},{160,224},{192,128},{224,1... | collective-permute-start | bytes 24584 | tf_op jit(solution)/shard_map/ppermute | solution.py:362
  118.6 12.9 %copy-start.4 = (f32[8,128]{1,0:T(8,128)S(1)}, f32[8,128]{1,0:T(8,128)}, u32[]{:S(2)}) copy-start(f32[8,128]{1,0:T(8,128)} %param.17) | copy-start | bytes 12292
  118.6 19.7 %copy-start.7 = (s32[1,8]{1,0:T(1,128)S(1)}, s32[1,8]{1,0:T(1,128)}, u32[]{:S(2)}) copy-start(s32[1,8]{1,0:T(1,128)} %param.11) | copy-start | bytes 100
  118.6 37.6 %all-to-all-start.3 = ((bf16[16,8,64,128]{3,2,1,0:T(8,128)(2,1)}), bf16[16,8,64,128]{3,2,1,0:T(8,128)(2,1)S(1)}, u32[]{:S(2)}, u32[]{:S(2)}) async-start(bf16[16,8,64,128]{3,2,1,0:T(8,128)(2,1)} %select.7), calls=%async_computation.3 | async-start | bytes 4194304 | tf_op jit(solution)/shard_map/all_to_all | solution.py:451
  124.5 6.7 %collective-permute-start.10 = (f32[16,128]{1,0:T(8,128)S(1)}, f32[16,128]{1,0:T(8,128)S(1)}, u32[]{:S(2)}, u32[]{:S(2)}) collective-permute-start(f32[16,128]{1,0:T(8,128)S(1)} %add.54), channel_id=1, source_target_pairs={{0,224},{32,192},{64,160},{96,128},{128,96},{160,64},{192,32},{224... | collective-permute-start | bytes 24584 | tf_op jit(solution)/shard_map/ppermute | solution.py:362
  131.6 26.8 %copy-start.2 = (f32[8,128]{1,0:T(8,128)}, f32[8,128]{1,0:T(8,128)S(1)}, u32[]{:S(2)}) copy-start(f32[8,128]{1,0:T(8,128)S(1)} %get-tuple-element.26) | copy-start | bytes 12292
  131.6 6.9 %collective-permute-start.11 = (f32[8,128]{1,0:T(8,128)S(1)}, f32[8,128]{1,0:T(8,128)S(1)}, u32[]{:S(2)}, u32[]{:S(2)}) collective-permute-start(f32[8,128]{1,0:T(8,128)S(1)} %get-tuple-element.26), channel_id=1, source_target_pairs={{0,34},{1,35},{2,32},{3,33},{4,38},{5,39},{6,36},{7,37},{8,42},{9,... | collective-permute-start | bytes 12296 | tf_op jit(solution)/shard_map/ppermute | solution.py:373
  134.4 6.1 %collective-permute-start.12 = (f32[8,128]{1,0:T(8,128)S(1)}, f32[8,128]{1,0:T(8,128)S(1)}, u32[]{:S(2)}, u32[]{:S(2)}) collective-permute-start(f32[8,128]{1,0:T(8,128)S(1)} %get-tuple-element.26), channel_id=1, source_target_pairs={{0,36},{1,37},{2,38},{3,39},{4,32},{5,33},{6,34},{7,35},{8,44},{9,... | collective-permute-start | bytes 12296 | tf_op jit(solution)/shard_map/ppermute | solution.py:373
  136.7 5.8 %collective-permute-start.13 = (f32[8,128]{1,0:T(8,128)S(1)}, f32[8,128]{1,0:T(8,128)S(1)}, u32[]{:S(2)}, u32[]{:S(2)}) collective-permute-start(f32[8,128]{1,0:T(8,128)S(1)} %get-tuple-element.26), channel_id=1, source_target_pairs={{0,38},{1,39},{2,36},{3,37},{4,34},{5,35},{6,32},{7,33},{8,46},{9,... | collective-permute-start | bytes 12296 | tf_op jit(solution)/shard_map/ppermute | solution.py:373
  142.5 9.2 %collective-permute-start.14 = (f32[32,128]{1,0:T(8,128)S(1)}, f32[32,128]{1,0:T(8,128)S(1)}, u32[]{:S(2)}, u32[]{:S(2)}) collective-permute-start(f32[32,128]{1,0:T(8,128)S(1)} %pad_maximum_fusion), channel_id=1, source_target_pairs={{0,40},{1,41},{2,42},{3,43},{4,44},{5,45},{6,46},{7,47},{8,32},{9,... | collective-permute-start | bytes 49160 | tf_op jit(solution)/shard_map/ppermute | solution.py:373
  145.3 6.4 %collective-permute-start.15 = (f32[32,128]{1,0:T(8,128)S(1)}, f32[32,128]{1,0:T(8,128)S(1)}, u32[]{:S(2)}, u32[]{:S(2)}) collective-permute-start(f32[32,128]{1,0:T(8,128)S(1)} %pad_maximum_fusion), channel_id=1, source_target_pairs={{0,48},{1,49},{2,50},{3,51},{4,52},{5,53},{6,54},{7,55},{8,56},{9,... | collective-permute-start | bytes 49160 | tf_op jit(solution)/shard_map/ppermute | solution.py:373
  150.3 5.8 %collective-permute-start.16 = (f32[32,128]{1,0:T(8,128)S(1)}, f32[32,128]{1,0:T(8,128)S(1)}, u32[]{:S(2)}, u32[]{:S(2)}) collective-permute-start(f32[32,128]{1,0:T(8,128)S(1)} %pad_maximum_fusion), channel_id=1, source_target_pairs={{0,56},{1,57},{2,58},{3,59},{4,60},{5,61},{6,62},{7,63},{8,48},{9,... | collective-permute-start | bytes 49160 | tf_op jit(solution)/shard_map/ppermute | solution.py:373
